TPU v7x, 32 devices: a whole 2x2x4 slice. The times are simulated.
32 devices in a mesh: az: 4 (over y, x), rng: 8 (over z, core).
Axes of the slice: x: 2, y: 2, z: 4, core: 2. Of those that a mesh axis runs over, the one named last changes fastest.
Arguments:
- echoes: bfloat16 [2, 256, 32, 1024], P(None, 'az', None, 'rng'), may hold values from -12 to 12
- arc_start: int32 [64], replicated, may hold values from 0 to 255, as said below
- arc_offsets: int32 [64, 16], replicated, may hold values from 0 to 63, as said below
- doppler_bins: int32 [64, 16], replicated, may hold values from 0 to 31
- steer_angles: float32 [64, 16], replicated, may hold values from -3.140625 to 3.140625
- train_mask: int32 [64, 8], P('az', 'rng'), may hold values from 0 to 1, as said below
Outputs:
- smoothed: float32 [64, 16, 1024], P('az', None, 'rng')
Inputs may be any that keep to these rules, and one draw needn't show every extreme that they name: `arc_start`: beam b's arc begins at column (b * 4 - 64 / 2 + j) mod 256 for some j with 0 <= j < 4. `arc_offsets`: each row holds 16 distinct offsets, ascending. `train_mask`: the last block of every beam is a training block.
All inputs are finite; a program needn't handle non-finite values.
Results may differ from a plain program's by a relative error of at most 0.0035.
Values may be sent and summed in bfloat16 or wider, within the bound.
A program may use at most 64 MiB of HBM per device.

v0:
```python
import jax
import jax.numpy as jnp
from jax import lax
from jax.sharding import PartitionSpec as P

COLS = 256
ARC = 64
BINS = 3
BEAMS = 64
BLK = 128


LOADING = 0.1


def with_halo(block, sides, width, periodic):
    for axis, dim in sides:
        count = lax.axis_size(axis)
        forward = [(i, i + 1) for i in range(count - 1)]
        if periodic:
            forward.append((count - 1, 0))
        backward = [(target, source) for source, target in forward]
        low = lax.ppermute(
            lax.slice_in_dim(block, block.shape[dim] - width, None, axis=dim), axis, forward
        )
        high = lax.ppermute(lax.slice_in_dim(block, 0, width, axis=dim), axis, backward)
        block = jnp.concatenate([low, block, high], axis=dim)
    return block


def doppler_table(num_pulses):
    freq_ids = jnp.arange(num_pulses, dtype=jnp.int32)
    phase_steps = freq_ids[:, None] * freq_ids[None, :] % num_pulses
    phase_angle = -2.0 * jnp.pi / num_pulses * phase_steps.astype(jnp.float32)
    return (jnp.cos(phase_angle).astype(jnp.bfloat16), jnp.sin(phase_angle).astype(jnp.bfloat16))


def snapshot(beam_cols, centers, beam_angle, table_re, table_im):
    num_sel = beam_cols.shape[1]
    num_pulses = beam_cols.shape[2]
    num_cells = beam_cols.shape[3]
    num_chan = centers.shape[0]
    bin_ids = (
        (centers[:, None] + jnp.arange(BINS, dtype=jnp.int32)[None, :] - BINS // 2) % num_pulses
    ).reshape(-1)
    bin_pick = (jnp.arange(num_pulses, dtype=jnp.int32)[None, :] == bin_ids[:, None]).astype(
        jnp.bfloat16
    )
    wt_real = jnp.dot(bin_pick, table_re, preferred_element_type=jnp.float32).astype(jnp.bfloat16)
    wt_imag = jnp.dot(bin_pick, table_im, preferred_element_type=jnp.float32).astype(jnp.bfloat16)
    stacked_table = jnp.concatenate(
        [jnp.concatenate([wt_real, -wt_imag], 1), jnp.concatenate([wt_imag, wt_real], 1)], 0
    )
    flat_cols = jnp.transpose(beam_cols, (0, 2, 1, 3)).reshape(2 * num_pulses, num_sel * num_cells)
    spectrum = jnp.dot(stacked_table, flat_cols, preferred_element_type=jnp.float32).reshape(
        2, num_chan, BINS, num_sel, num_cells
    )
    cosine = jnp.cos(beam_angle)[None, None, :, None]
    sine_part = jnp.sin(beam_angle)[None, None, :, None]
    part_real = cosine * spectrum[0] - sine_part * spectrum[1]
    part_imag = sine_part * spectrum[0] + cosine * spectrum[1]
    joined = jnp.concatenate(
        [
            part_real.reshape(num_chan, BINS * num_sel, num_cells),
            part_imag.reshape(num_chan, BINS * num_sel, num_cells),
        ],
        1,
    )
    return joined.astype(jnp.bfloat16)


def beam_snapshots(column_block, col_index, centers, angles_all, table_re, table_im):

    def per_beam(packed):
        index_row, center_row, beam_angle = packed
        beam_cols = jnp.take(column_block, index_row, axis=1)
        return snapshot(beam_cols, center_row, beam_angle, table_re, table_im)

    return lax.map(per_beam, (col_index, centers, angles_all))


def weights_from_blocks(block_a, block_b, train_count):
    dof_size = block_a.shape[0]
    embedded = (
        jnp.concatenate(
            [jnp.concatenate([block_a, -block_b], 1), jnp.concatenate([block_b, block_a], 1)], 0
        )
        / train_count
    )
    loading_level = LOADING * jnp.trace(block_a) / (train_count * dof_size)
    embedded = embedded + loading_level * jnp.eye(2 * dof_size, dtype=jnp.float32)
    factor = jnp.linalg.cholesky(embedded)
    steering = (
        jnp.arange(2 * dof_size, dtype=jnp.int32)[:, None] // dof_size
        == jnp.arange(2, dtype=jnp.int32)[None, :]
    ).astype(jnp.float32)
    solved = jax.scipy.linalg.cho_solve((factor, True), steering)
    quiescent = jnp.sum(solved[:dof_size, 0])
    return (solved.T, quiescent)


def body(echoes, arc_start, arc_offsets, doppler_bins, steer_angles, train_mask):
    columns = echoes.shape[1]
    num_pulses = echoes.shape[2]
    cycle_size = lax.axis_size("az")
    cycle_pos = lax.axis_index("az")
    beam_count = BEAMS // cycle_size
    chan_count = doppler_bins.shape[1]
    item_count = beam_count * chan_count
    table_re, table_im = doppler_table(num_pulses)
    own_beams = cycle_pos * beam_count + jnp.arange(beam_count, dtype=jnp.int32)
    extended = with_halo(echoes, (("az", 1),), ARC // 2, True)
    arc_first = (arc_start[own_beams] - cycle_pos * columns + ARC // 2) % COLS
    col_index = arc_first[:, None] + arc_offsets[own_beams]
    snapshots = beam_snapshots(
        extended, col_index, doppler_bins[own_beams], steer_angles[own_beams], table_re, table_im
    )
    block_count = train_mask.shape[1]
    cell_mask = (
        jnp.broadcast_to(train_mask[:, :, None], (beam_count, block_count, BLK))
        .reshape(beam_count, block_count * BLK)
        .astype(jnp.bfloat16)
    )
    gram_local = jnp.einsum(
        "bkdr,bker->bkde",
        snapshots * cell_mask[:, None, None, :],
        snapshots,
        preferred_element_type=jnp.float32,
    )
    count_beam = (BLK * jnp.sum(train_mask, axis=1)).astype(jnp.float32)
    count_local = jnp.broadcast_to(count_beam[:, None], (beam_count, chan_count)).reshape(
        item_count
    )
    dof_size = gram_local.shape[2] // 2
    gram_items = gram_local.reshape(item_count, 2 * dof_size, 2 * dof_size)
    gram_part, count_part = (
        lax.psum_scatter(gram_items, "rng", scatter_dimension=0, tiled=True),
        lax.psum_scatter(count_local, "rng", scatter_dimension=0, tiled=True),
    )
    block_a = gram_part[:, :dof_size, :dof_size] + gram_part[:, dof_size:, dof_size:]
    block_b = gram_part[:, dof_size:, :dof_size] - gram_part[:, :dof_size, dof_size:]
    solved_part, quiet_part = jax.vmap(weights_from_blocks)(block_a, block_b, count_part)
    solved_all, quiet_all = (
        lax.all_gather(solved_part, "rng", axis=0, tiled=True),
        lax.all_gather(quiet_part, "rng", axis=0, tiled=True),
    )
    adapted = solved_all.reshape(beam_count, chan_count, 2, 2 * dof_size).astype(jnp.bfloat16)
    quiescent = quiet_all.reshape(beam_count, chan_count)
    projected = jnp.einsum(
        "bkcd,bkdr->bkcr", adapted, snapshots, preferred_element_type=jnp.float32
    )
    power_map = (
        projected[:, :, 0] * projected[:, :, 0] + projected[:, :, 1] * projected[:, :, 1]
    ) / quiescent[:, :, None]
    range_ext = with_halo(power_map, (("rng", 2),), 1, False)
    row_sums = range_ext[:, :, :-2] + range_ext[:, :, 1:-1] + range_ext[:, :, 2:]
    beam_ext = with_halo(row_sums, (("az", 0),), 1, True)
    smoothed = (beam_ext[:-2] + beam_ext[1:-1] + beam_ext[2:]) / 9.0
    return smoothed


def solution(mesh):
    return jax.shard_map(
        body,
        mesh=mesh,
        in_specs=(P(None, "az", None, "rng"), P(), P(), P(), P(), P("az", "rng")),
        out_specs=P("az", None, "rng"),
        check_vma=False,
    )
```

profile of v0, /device:TPU:0, one launch (start us, length us, event | category | flops | bytes accessed | tf_op | source)
XLA Modules:
  0.0 789.7 jit_solution(943671117625869362)
XLA Ops:
  8.0 3.0 collective-permute-start
  14.8 9.9 %collective-permute-done = bf16[2,32,32,128]{3,2,1,0:T(8,128)(2,1)S(1)} collective-permute-done((bf16[2,32,32,128]{3,2,1,0:T(8,128)(2,1)S(1)}, bf16[2,32,32,128]{3,2,1,0:T(8,128)(2,1)S(1)}, u32[]{:S(2)}, u32[]{:S(2)}) %collective-permute-start) | collective-permute-done | bytes 524320 | tf_op jit(solution)/shard_map/ppermute | solution.py:23
  25.5 10.0 %collective-permute-done.1 = bf16[2,32,32,128]{3,2,1,0:T(8,128)(2,1)} collective-permute-done((bf16[2,32,32,128]{3,2,1,0:T(8,128)(2,1)S(1)}, bf16[2,32,32,128]{3,2,1,0:T(8,128)(2,1)}, u32[]{:S(2)}, u32[]{:S(2)}) %collective-permute-start.1) | collective-permute-done | bytes 524320 | tf_op jit(solution)/shard_map/ppermute | solution.py:26
  36.9 55.2 %while.13 = (s32[]{:T(128)}, bf16[16,16,96,128]{3,2,1,0:T(8,128)(2,1)}, f32[16,16]{1,0:T(8,128)S(1)}, s32[16,16]{1,0:T(8,128)S(1)}, s32[16,16]{1,0:T(8,128)S(1)}...) while((s32[]{:T(128)}, bf16[16,16,96,128]{3,2,1,0:T(8,128)(2,1)}, f32[16,16]{1,0:T(8,128)S(1)}, ...), condition=%wide.region_1.2_spmd.clone, body=%wide.region_0.1_spmd.clone.sunk | while | flops 27155712 | bytes 7760125 | solution.py:79
  92.1 13.5 %fusion.38 = f32[16,16,96,96]{2,3,1,0:T(8,128)} fusion(bf16[16,16,96,128]{3,2,1,0:T(8,128)(2,1)} %get-tuple-element.108, bf16[16]{0:T(256)(128)(2,1)S(1)} %get-tuple-element.161), kind=kOutput, calls=%fused_computation.64 | convolution fusion | flops 607125504 | bytes 15728672 | tf_op jit(solution)/shard_map/bkdr,bker->bkde/dot_general | solution.py:124
  108.4 16.6 %all-reduce.1 = f32[256]{0:T(256)S(1)} all-reduce(f32[256]{0:T(256)S(1)} %reshape.287), channel_id=3, replica_groups=mesh['az'=4,'rng'=8] {'rng'}, use_global_device_ids=true, to_apply=%region_3.4.clone | all-reduce | flops 256 | bytes 2048
  125.1 110.4 %reduce-scatter.2.cloned.1.call-done = f32[32,96,96]{1,2,0:T(8,128)} async-done(((f32[256,96,96]{1,2,0:T(8,128)}), f32[32,96,96]{1,2,0:T(8,128)}) %reduce-scatter.2.cloned.1.call-update) | async-done | bytes 1179664 | tf_op jit(solution)/shard_map/reduce_scatter | solution.py:137
  235.5 2.8 fusion.54
  238.4 1.7 fusion.41
  240.1 3.0 copy.32
  243.2 3.3 fusion.42
  246.5 282.0 %custom-call.11 = f32[32,96,96]{2,1,0:T(8,128)S(1)} custom-call(f32[32,96,96]{2,1,0:T(8,128)} %fusion.42), custom_call_target="Cholesky" | custom-call | tf_op jit(solution)/shard_map/vmap(jit(cholesky))/cholesky | solution.py:92
  528.4 2.9 copy.33
  531.4 5.1 select_reduce_fusion
  536.5 3.8 select_bitcast_fusion.1
  540.3 190.0 %custom-call.12 = f32[32,1,96,96]{0,2,3,1:T(8,128)} custom-call(f32[32,1,96,96]{0,3,2,1:T(8,128)} %select_bitcast_fusion.1), custom_call_target="InvertDiagBlocksLowerTriangular" | custom-call | tf_op jit(solution)/shard_map/vmap(jit(_cho_solve))/triangular_solve | solution.py:97
  730.3 3.7 copy.36
  734.0 2.5 fusion.49
  738.4 14.2 %all_gather.6 = bf16[256,2,96]{2,1,0:T(2,128)(2,1)S(1)} all-gather(bf16[32,2,96]{2,1,0:T(2,128)(2,1)S(1)} %bitcast_convert_fusion), channel_id=1, replica_groups=mesh['az'=4,'rng'=8] {'rng'}, dimensions={0}, use_global_device_ids=true | all-gather | bytes 110592 | tf_op jit(solution)/shard_map/all_gather | solution.py:144
  752.5 4.5 fusion.62
  757.5 14.5 %all-reduce = f32[256]{0:T(256)S(1)} all-reduce(f32[256]{0:T(256)S(1)} %dynamic-update-slice.3), channel_id=1, replica_groups=mesh['az'=4,'rng'=8] {'rng'}, use_global_device_ids=true, to_apply=%add | all-reduce | flops 256 | bytes 2048
  774.9 1.9 collective-permute-done.3
  777.0 1.5 collective-permute-start.4
  780.0 1.6 collective-permute-done.4
  (433 shorter events, 70.8 us)
Async XLA Ops:
  6.5 5.5 copy-start
  6.5 28.9 %copy-start.2 = (bf16[2,64,32,128]{3,2,1,0:T(8,128)(2,1)S(1)}, bf16[2,64,32,128]{3,2,1,0:T(8,128)(2,1)}, u32[]{:S(2)}) copy-start(bf16[2,64,32,128]{3,2,1,0:T(8,128)(2,1)} %param.8) | copy-start | bytes 3145732
  6.5 6.2 copy-start.4
  6.5 6.8 copy-start.5
  6.5 7.5 copy-start.6
  6.5 8.1 %copy-start.8 = (s32[16,1]{0,1:T(1,128)S(1)}, s32[16,1]{0,1:T(1,128)}, u32[]{:S(2)}) copy-start(s32[16,1]{0,1:T(1,128)} %param.13) | copy-start | bytes 196
  6.6 228.9 %reduce-scatter.2.cloned.1.call-start = ((), (), s32[]{:S(2)}) async-start(), calls=%async_computation.1 | async-start | bytes 14155776 | tf_op jit(solution)/shard_map/reduce_scatter | solution.py:137
  8.0 16.7 %collective-permute-start = (bf16[2,32,32,128]{3,2,1,0:T(8,128)(2,1)S(1)}, bf16[2,32,32,128]{3,2,1,0:T(8,128)(2,1)S(1)}, u32[]{:S(2)}, u32[]{:S(2)}) collective-permute-start(bf16[2,32,32,128]{3,2,1,0:T(8,128)(2,1)S(1)} %get-tuple-element.152), channel_id=1, source_target_pairs={{0,8},{8,16},{16,24},{24,0},{1,9},{9,17},{17,25},{25,1},{2,10},{10... | collective-permute-start | bytes 1572872 | tf_op jit(solution)/shard_map/ppermute | solution.py:23
  11.0 24.5 %collective-permute-start.1 = (bf16[2,32,32,128]{3,2,1,0:T(8,128)(2,1)S(1)}, bf16[2,32,32,128]{3,2,1,0:T(8,128)(2,1)}, u32[]{:S(2)}, u32[]{:S(2)}) collective-permute-start(bf16[2,32,32,128]{3,2,1,0:T(8,128)(2,1)S(1)} %get-tuple-element.153), channel_id=1, source_target_pairs={{8,0},{16,8},{24,16},{0,24},{9,1},{17,9},{25,17},{1,25},{10,2},{18... | collective-permute-start | bytes 1572872 | tf_op jit(solution)/shard_map/ppermute | solution.py:26
  24.7 0.8 copy-start.3
  105.7 0.7 copy-start.7
  531.4 5.1 copy-start.1
  772.3 2.6 collective-permute-start.2
  773.6 3.2 collective-permute-start.3
  777.0 4.6 collective-permute-start.4
  778.6 3.7 collective-permute-start.5
Sparse Core Ops, SparseCore 0:
  105.8 129.6 reduce-scatter.1
where the time goes:
time: 791 us; the launch traced here: 790 us
  other arithmetic  511 us (65%)
  waiting for transfers between devices  134 us (17%)
  blocking collectives  45.3 us (6%)
  local copies, waits for them, and re-layouts  36.8 us (5%)
  matrix products  36.6 us (5%)
  between operations  14.9 us (2%)
  starting transfers between devices  9.64 us (1%)
    another operation x4, other arithmetic, weights_from_blocks(): factor = jnp.linalg.cholesky(embedded)  287 us
    another operation x3, other arithmetic, weights_from_blocks(): solved = jax.scipy.linalg.cho_solve((factor, True), steering)  194 us
    reduce_scatter x1, waiting for transfers between devices, body(): lax.psum_scatter(gram_items, 'rng', scatter_dimension=0, tiled=True)  110 us
    unnamed x2, blocking collectives  31.1 us
  transfers between devices with their start and end apart: 7, of which 6 were waited for; matrix products, arithmetic and copies ran while one was open for 0% of the time, Pallas kernels for 0%

commit v1 on v0

v1 whole, which is shorter than its diff:
```python
import functools

import jax
import jax.numpy as jnp
from jax import lax
from jax.experimental import pallas as pl
from jax.experimental.pallas import tpu as pltpu
from jax.sharding import PartitionSpec as P

COLS = 256
ARC = 64
BINS = 3
BEAMS = 64
BLK = 128
LOADING = 0.1
VMEM_LIMIT = 48 << 20


def with_halo(block, sides, width, periodic):
    for axis, dim in sides:
        count = lax.axis_size(axis)
        forward = [(i, i + 1) for i in range(count - 1)]
        if periodic:
            forward.append((count - 1, 0))
        backward = [(target, source) for source, target in forward]
        low = lax.ppermute(
            lax.slice_in_dim(block, block.shape[dim] - width, None, axis=dim), axis, forward
        )
        high = lax.ppermute(lax.slice_in_dim(block, 0, width, axis=dim), axis, backward)
        block = jnp.concatenate([low, block, high], axis=dim)
    return block


def doppler_table(num_pulses):
    freq_ids = jnp.arange(num_pulses, dtype=jnp.int32)
    phase_steps = freq_ids[:, None] * freq_ids[None, :] % num_pulses
    phase_angle = -2.0 * jnp.pi / num_pulses * phase_steps.astype(jnp.float32)
    return (jnp.cos(phase_angle).astype(jnp.bfloat16), jnp.sin(phase_angle).astype(jnp.bfloat16))


def snap_gram_kernel(
    col_ref, bins_ref, cos_ref, sin_ref, ext_ref, table_ref, mask_ref, v_ref, gram_ref
):
    beam = pl.program_id(0)
    pulses = ext_ref.shape[2]
    cells = ext_ref.shape[3]
    num_sel = col_ref.shape[1]
    num_chan = bins_ref.shape[1]
    table = table_ref[...]
    parts_re, parts_im = [], []
    for j in range(num_sel):
        col = col_ref[beam, j]
        data = jnp.concatenate([ext_ref[0, col], ext_ref[1, col]], axis=0)
        spec = jnp.dot(table, data, preferred_element_type=jnp.float32)
        cosine = cos_ref[beam, j]
        sine = sin_ref[beam, j]
        spec_re = spec[:pulses]
        spec_im = spec[pulses:]
        parts_re.append(cosine * spec_re - sine * spec_im)
        parts_im.append(sine * spec_re + cosine * spec_im)
    for part, pieces in enumerate((parts_re, parts_im)):
        stacked = jnp.swapaxes(jnp.stack(pieces, 0), 0, 1)
        v_ref[0, part] = stacked.astype(jnp.bfloat16)
    dof = BINS * num_sel
    mask_row = mask_ref[0]
    row = lax.broadcasted_iota(jnp.int32, (dof, dof), 0)
    colm = lax.broadcasted_iota(jnp.int32, (dof, dof), 1)
    lower = row >= colm
    packed = []
    for k in range(num_chan):
        centre = bins_ref[beam, k]
        ids = [(centre + (q - BINS // 2 + pulses)) % pulses for q in range(BINS)]
        u_re = jnp.concatenate([v_ref[0, 0, f] for f in ids], 0)
        u_im = jnp.concatenate([v_ref[0, 1, f] for f in ids], 0)
        right = jnp.concatenate([u_re, u_im], 1)
        m_re = u_re * mask_row
        m_im = u_im * mask_row
        left = jnp.concatenate(
            [jnp.concatenate([m_re, m_im], 1), jnp.concatenate([m_im, -m_re], 1)], 0
        )
        both = lax.dot_general(
            left, right, (((1,), (1,)), ((), ())), preferred_element_type=jnp.float32
        )
        packed.append(jnp.where(lower, both[:dof], both[dof:]))
    gram_ref[0] = jnp.concatenate(packed, 1)


def solve_kernel(hr_in, hi_in, out_ref, hr, hi, xr, xi):
    dof = hr_in.shape[0]
    lanes = hr_in.shape[2]
    nb = dof // 8
    hr[:, :dof, :] = hr_in[...]
    hi[:, :dof, :] = hi_in[...]
    hr[:, dof:, :] = jnp.ones((dof, 8, lanes), jnp.float32)
    hi[:, dof:, :] = jnp.zeros((dof, 8, lanes), jnp.float32)
    xr[...] = jnp.zeros_like(xr)
    xi[...] = jnp.zeros_like(xi)
    trace = jnp.zeros((1, lanes), jnp.float32)
    for i in range(dof):
        trace = trace + hr[i, i : i + 1, :]
    load = (LOADING / dof) * trace
    for i in range(dof):
        hr[i, i : i + 1, :] = hr[i, i : i + 1, :] + load
    sub = lax.broadcasted_iota(jnp.int32, (8, lanes), 0)

    for kb in range(nb):

        def step(k, carry, kb=kb):
            pivot = 1.0 / hr[k, pl.ds(k, 1), :]
            rr = [hr[k, 8 * b : 8 * b + 8, :] for b in range(kb, nb + 1)]
            ri = [hi[k, 8 * b : 8 * b + 8, :] for b in range(kb, nb + 1)]
            for ib in range(kb, nb):
                fr = rr[ib - kb] * pivot
                fi = -ri[ib - kb] * pivot
                if ib == kb:
                    live = sub + 8 * kb > k
                    fr = jnp.where(live, fr, 0.0)
                    fi = jnp.where(live, fi, 0.0)
                for s in range(8):
                    i = 8 * ib + s
                    cr = jnp.broadcast_to(fr[s : s + 1], (8, lanes))
                    ci = jnp.broadcast_to(fi[s : s + 1], (8, lanes))
                    for b in range(ib, nb + 1):
                        pr, pi = rr[b - kb], ri[b - kb]
                        sl = slice(8 * b, 8 * b + 8)
                        hr[i, sl, :] = hr[i, sl, :] - (cr * pr - ci * pi)
                        hi[i, sl, :] = hi[i, sl, :] - (cr * pi + ci * pr)
            return carry

        lax.fori_loop(8 * kb, 8 * kb + 8, step, 0)

    for ib in reversed(range(nb)):

        def back(t, carry, ib=ib):
            i = 8 * ib + 7 - t
            sr = jnp.zeros((8, lanes), jnp.float32)
            si = jnp.zeros((8, lanes), jnp.float32)
            for b in range(ib, nb):
                sl = slice(8 * b, 8 * b + 8)
                ar, ai = hr[i, sl, :], hi[i, sl, :]
                br, bi = xr[sl, :], xi[sl, :]
                sr = sr + (ar * br - ai * bi)
                si = si + (ar * bi + ai * br)
            pivot = 1.0 / hr[i, pl.ds(i, 1), :]
            top_r = hr[i, dof : dof + 1, :]
            top_i = hi[i, dof : dof + 1, :]
            xr[pl.ds(i, 1), :] = (top_r - jnp.sum(sr, 0, keepdims=True)) * pivot
            xi[pl.ds(i, 1), :] = (top_i - jnp.sum(si, 0, keepdims=True)) * pivot
            return carry

        lax.fori_loop(0, 8, back, 0)
    out_ref[:dof, :] = xr[...]
    out_ref[dof : 2 * dof, :] = xi[...]
    out_ref[2 * dof :, :] = jnp.broadcast_to(jnp.sum(xr[...], 0, keepdims=True), (8, lanes))


def power_kernel(w_ref, quiet_ref, v_ref, out_ref):
    num_chan = out_ref.shape[1]
    flat = v_ref[0].reshape(w_ref.shape[2], v_ref.shape[4])
    proj = jnp.dot(w_ref[0], flat, preferred_element_type=jnp.float32)
    p0 = proj[:num_chan]
    p1 = proj[num_chan:]
    out_ref[0] = (p0 * p0 + p1 * p1) / quiet_ref[0]


def body(echoes, arc_start, arc_offsets, doppler_bins, steer_angles, train_mask):
    columns = echoes.shape[1]
    num_pulses = echoes.shape[2]
    cells = echoes.shape[3]
    num_sel = arc_offsets.shape[1]
    chan_count = doppler_bins.shape[1]
    cycle_size = lax.axis_size("az")
    cycle_pos = lax.axis_index("az")
    rng_size = lax.axis_size("rng")
    beam_count = BEAMS // cycle_size
    item_count = beam_count * chan_count
    dof = BINS * num_sel
    table_re, table_im = doppler_table(num_pulses)
    table = jnp.concatenate(
        [jnp.concatenate([table_re, -table_im], 1), jnp.concatenate([table_im, table_re], 1)], 0
    )

    def own(x):
        return lax.dynamic_slice_in_dim(x, cycle_pos * beam_count, beam_count, axis=0)

    extended = with_halo(echoes, (("az", 1),), ARC // 2, True)
    arc_first = (own(arc_start) - cycle_pos * columns + ARC // 2) % COLS
    col_index = arc_first[:, None] + own(arc_offsets)
    bins_own = own(doppler_bins)
    angles = own(steer_angles)
    block_count = train_mask.shape[1]
    cell_mask = (
        jnp.broadcast_to(train_mask[:, :, None], (beam_count, block_count, BLK))
        .reshape(beam_count, 1, block_count * BLK)
        .astype(jnp.bfloat16)
    )
    smem = pl.BlockSpec(memory_space=pltpu.SMEM)
    ext_cols = extended.shape[1]
    v_all, gram = pl.pallas_call(
        snap_gram_kernel,
        grid=(beam_count,),
        in_specs=[
            smem,
            smem,
            smem,
            smem,
            pl.BlockSpec((2, ext_cols, num_pulses, cells), lambda b: (0, 0, 0, 0)),
            pl.BlockSpec(table.shape, lambda b: (0, 0)),
            pl.BlockSpec((1, 1, cells), lambda b: (b, 0, 0)),
        ],
        out_specs=[
            pl.BlockSpec((1, 2, num_pulses, num_sel, cells), lambda b: (b, 0, 0, 0, 0)),
            pl.BlockSpec((1, dof, chan_count * dof), lambda b: (b, 0, 0)),
        ],
        out_shape=[
            jax.ShapeDtypeStruct((beam_count, 2, num_pulses, num_sel, cells), jnp.bfloat16),
            jax.ShapeDtypeStruct((beam_count, dof, chan_count * dof), jnp.float32),
        ],
        compiler_params=pltpu.CompilerParams(vmem_limit_bytes=VMEM_LIMIT),
        name="snap_gram",
    )(col_index, bins_own, jnp.cos(angles), jnp.sin(angles), extended, table, cell_mask)

    per = item_count // rng_size
    if per < chan_count:
        split = chan_count // per
        gram = gram.reshape(beam_count, dof, split, per * dof)
        gram = jnp.swapaxes(gram, 1, 2).reshape(beam_count * split, dof, per * dof)
        width = per
    else:
        width = chan_count
    part = lax.psum_scatter(gram, "rng", scatter_dimension=0, tiled=True)
    lead = part.shape[0]
    mats = part.reshape(lead, dof, width, dof).transpose(1, 3, 0, 2).reshape(dof, dof, per)
    flip = jnp.swapaxes(mats, 0, 1)
    ids = jnp.arange(dof, dtype=jnp.int32)
    row, col = ids[:, None, None], ids[None, :, None]
    h_re = jnp.where(row >= col, mats, flip)
    h_im = jnp.where(row < col, mats, jnp.where(row > col, -flip, 0.0))
    vm = pltpu.VMEM
    solved = pl.pallas_call(
        solve_kernel,
        out_shape=jax.ShapeDtypeStruct((2 * dof + 8, per), jnp.float32),
        scratch_shapes=[
            vm((dof, dof + 8, per), jnp.float32),
            vm((dof, dof + 8, per), jnp.float32),
            vm((dof, per), jnp.float32),
            vm((dof, per), jnp.float32),
        ],
        compiler_params=pltpu.CompilerParams(vmem_limit_bytes=VMEM_LIMIT),
        name="solve",
    )(h_re, h_im)
    body_size = (2 * dof + 1) * per
    local_count = (BLK * jnp.sum(train_mask, axis=1)).astype(jnp.float32)
    payload = jnp.concatenate([solved[: 2 * dof + 1].reshape(body_size), local_count])
    gathered = lax.all_gather(payload, "rng", axis=0)
    count = jnp.sum(gathered[:, body_size:], axis=0)
    sol = gathered[:, :body_size].reshape(rng_size, 2 * dof + 1, per)
    sol = jnp.swapaxes(sol, 1, 2).reshape(beam_count, chan_count, 2 * dof + 1)
    sol = sol * count[:, None, None]
    quiet = sol[:, :, 2 * dof :]
    adapted = sol[:, :, : 2 * dof].astype(jnp.bfloat16)
    adapted = adapted.reshape(beam_count, chan_count, 2, BINS, 1, num_sel)
    freq = jnp.arange(num_pulses, dtype=jnp.int32)
    spread = jnp.zeros((beam_count, chan_count, 2, num_pulses, num_sel), jnp.bfloat16)
    for q in range(BINS):
        hit = ((bins_own + (q - BINS // 2)) % num_pulses)[:, :, None] == freq
        spread = jnp.where(hit[:, :, None, :, None], adapted[:, :, :, q], spread)
    taps = num_pulses * num_sel
    spread = spread.reshape(beam_count, chan_count, 2, taps)
    w_re, w_im = spread[:, :, 0], spread[:, :, 1]
    weights = jnp.concatenate(
        [jnp.concatenate([w_re, w_im], 2), jnp.concatenate([-w_im, w_re], 2)], 1
    )
    power_map = pl.pallas_call(
        power_kernel,
        grid=(beam_count,),
        in_specs=[
            pl.BlockSpec((1, 2 * chan_count, 2 * taps), lambda b: (b, 0, 0)),
            pl.BlockSpec((1, chan_count, 1), lambda b: (b, 0, 0)),
            pl.BlockSpec((1, 2, num_pulses, num_sel, cells), lambda b: (b, 0, 0, 0, 0)),
        ],
        out_specs=pl.BlockSpec((1, chan_count, cells), lambda b: (b, 0, 0)),
        out_shape=jax.ShapeDtypeStruct((beam_count, chan_count, cells), jnp.float32),
        compiler_params=pltpu.CompilerParams(vmem_limit_bytes=VMEM_LIMIT),
        name="power",
    )(weights, quiet, v_all)
    range_ext = with_halo(power_map, (("rng", 2),), 1, False)
    row_sums = range_ext[:, :, :-2] + range_ext[:, :, 1:-1] + range_ext[:, :, 2:]
    beam_ext = with_halo(row_sums, (("az", 0),), 1, True)
    return (beam_ext[:-2] + beam_ext[1:-1] + beam_ext[2:]) / 9.0


def solution(mesh):
    return jax.shard_map(
        body,
        mesh=mesh,
        in_specs=(P(None, "az", None, "rng"), P(), P(), P(), P(), P("az", "rng")),
        out_specs=P("az", None, "rng"),
        check_vma=False,
    )
```

time: 791 us -> 213 us (0.27)
  other arithmetic: 511 us -> 4.04 us
  blocking collectives: 45.3 us -> 0 us
  matrix products: 36.6 us -> 0 us
  waiting for transfers between devices: 134 us -> 102 us
  Pallas kernels: 0 us -> 24.5 us
  local copies, waits for them, and re-layouts: 36.8 us -> 56 us
    another operation x7 -> x0, other arithmetic: 481 us -> none  [the longest x4 287 us: weights_from_blocks(): factor = jnp.linalg.cholesky(embedded)]
    reduce_scatter x1, waiting for transfers between devices: 110 us -> 36.1 us  [body(): part = lax.psum_scatter(gram, 'rng', scatter_dimension=0, tiled=True)]
    broadcast_in_dim x1 -> x13, local copies, waits for them, and re-layouts: 0.07 us -> 46.1 us  [the longest x12 46 us: body(): spread = jnp.where(hit[:, :, None, :, None], adapted[:, :, :, q], spread)]
    unnamed x1 -> x3, waiting for transfers between devices: 0.02 us -> 36.3 us
    dot_general x50 -> x0, matrix products: 32.6 us -> none  [the longest x1 13.5 us: body(): jnp.einsum('bkdr,bker->bkde', snapshots * cell_mask[:, None, None, :], sn...]
    unnamed x2 -> x0, blocking collectives: 31.1 us -> none
    pallas_call x0 -> x3, Pallas kernels: none -> 24.5 us  [the longest x1 14.2 us: body(): pl.pallas_call(snap_gram_kernel, grid=(beam_count,), in_specs=[smem, smem...]
    all_gather x1 -> x0, blocking collectives: 14.2 us -> none  [body(): lax.all_gather(solved_part, 'rng', axis=0, tiled=True)]
  transfers between devices with their start and end apart: 7 -> 8, of which waited for: 6 -> 7; matrix products, arithmetic and copies ran while one was open for 0% -> 8% of each run, Pallas kernels for 0% -> 0%
where the time goes in v1:
time: 213 us; the launch traced here: 211 us
  waiting for transfers between devices  102 us (48%)
  local copies, waits for them, and re-layouts  56 us (26%)
  Pallas kernels  24.5 us (12%)
  between operations  14.5 us (7%)
  starting transfers between devices  9.69 us (5%)
  other arithmetic  4.04 us (2%)
    broadcast_in_dim x12, local copies, waits for them, and re-layouts, body(): spread = jnp.where(hit[:, :, None, :, None], adapted[:, :, :, q], spread)  46 us
    unnamed x3, waiting for transfers between devices  36.3 us
    reduce_scatter x1, waiting for transfers between devices, body(): part = lax.psum_scatter(gram, 'rng', scatter_dimension=0, tiled=True)  36.1 us
    ppermute x3, waiting for transfers between devices, with_halo(): lax.ppermute(lax.slice_in_dim(block, 0, width, axis=dim), axis, backward)  16.4 us
    pallas_call x1, Pallas kernels, body(): pl.pallas_call(snap_gram_kernel, grid=(beam_count,), in_specs=[smem, smem...  14.2 us
    ppermute x3, waiting for transfers between devices, with_halo(): lax.ppermute(lax.slice_in_dim(block, block.shape[dim] - width, None, axis...  13.4 us
    pallas_call x1, Pallas kernels, body(): pl.pallas_call(solve_kernel, out_shape=jax.ShapeDtypeStruct((2 * dof + 8,...  7.55 us
    ppermute x3, starting transfers between devices, with_halo(): lax.ppermute(lax.slice_in_dim(block, block.shape[dim] - width, None, axis...  5.84 us
  transfers between devices with their start and end apart: 8, of which 7 were waited for; matrix products, arithmetic and copies ran while one was open for 8% of the time, Pallas kernels for 0%

profile of v1, /device:TPU:0, one launch (start us, length us, event | category | flops | bytes accessed | tf_op | source)
XLA Modules:
  0.0 210.9 jit_solution(1316831868240181832)
XLA Ops:
  8.0 3.0 %collective-permute-start = (bf16[2,32,32,128]{3,2,1,0:T(8,128)(2,1)S(1)}, bf16[2,32,32,128]{3,2,1,0:T(8,128)(2,1)S(1)}, u32[]{:S(2)}, u32[]{:S(2)}) collective-permute-start(bf16[2,32,32,128]{3,2,1,0:T(8,128)(2,1)S(1)} %get-tuple-element.11), channel_id=1, source_target_pairs={{0,8},{8,16},{16,24},{24,0},{1,9},{9,17},{17,25},{25,1},{2,10},{10... | collective-permute-start | bytes 1572872 | tf_op jit(solution)/shard_map/ppermute | solution.py:26
  13.0 11.8 %collective-permute-done = bf16[2,32,32,128]{3,2,1,0:T(8,128)(2,1)S(1)} collective-permute-done((bf16[2,32,32,128]{3,2,1,0:T(8,128)(2,1)S(1)}, bf16[2,32,32,128]{3,2,1,0:T(8,128)(2,1)S(1)}, u32[]{:S(2)}, u32[]{:S(2)}) %collective-permute-start) | collective-permute-done | bytes 524320 | tf_op jit(solution)/shard_map/ppermute | solution.py:26
  24.7 10.6 %collective-permute-done.1 = bf16[2,32,32,128]{3,2,1,0:T(8,128)(2,1)S(1)} collective-permute-done((bf16[2,32,32,128]{3,2,1,0:T(8,128)(2,1)S(1)}, bf16[2,32,32,128]{3,2,1,0:T(8,128)(2,1)S(1)}, u32[]{:S(2)}, u32[]{:S(2)}) %collective-permute-start.1) | collective-permute-done | bytes 524320 | tf_op jit(solution)/shard_map/ppermute | solution.py:29
  35.7 14.2 %snap_gram.1 = (bf16[16,2,32,16,128]{4,3,2,1,0:T(8,128)(2,1)}, f32[16,48,768]{2,1,0:T(8,128)}) custom-call(s32[16,16]{1,0:T(8,128)S(1)} %broadcast_add_fusion.col_ref, s32[16,16]{1,0:T(8,128)S(1)} %copy.29.bins_ref, f32[16,16]{1,0:T(8,128)S(1)} %get-tuple-element.26.cos_ref, f32[16,16]{1,0:T(8,128)S(1)} %get-tuple-element.25.sin_ref, ...), custom_call_target="tpu_custom_call" | custom-call | tf_op jit(solution)/shard_map/snap_gram/pallas_call | solution.py:199
  51.4 36.1 %reduce-scatter.2.cloned.1.call-done = f32[2,48,768]{2,1,0:T(8,128)} async-done(((f32[16,48,768]{2,1,0:T(8,128)}), f32[2,48,768]{2,1,0:T(8,128)}) %reduce-scatter.2.cloned.1.call-update) | async-done | bytes 294928 | tf_op jit(solution)/shard_map/reduce_scatter | solution.py:231
  91.2 7.6 %solve.1 = f32[104,32]{1,0:T(8,128)S(1)} custom-call(f32[48,48,32]{2,1,0:T(8,128)S(1)} %get-tuple-element.10.hr_in, f32[48,48,32]{2,1,0:T(8,128)S(1)} %get-tuple-element.9.hi_in), custom_call_target="tpu_custom_call" | custom-call | tf_op jit(solution)/shard_map/solve/pallas_call | solution.py:240
  100.0 1.4 broadcast_in_dim.120
  101.4 3.6 %broadcast_in_dim.121 = pred[16,16,512]{2,1,0:T(8,128)(4,1)S(1)} reshape(pred[16,16,32,16]{3,2,1,0:T(8,128)(4,1)S(1)} %broadcast_in_dim.120) | data formatting | bytes 262144 | tf_op jit(solution)/shard_map/jit(_where)/broadcast_in_dim | solution.py:267
  105.0 1.4 broadcast_in_dim.126
  106.4 3.6 %broadcast_in_dim.127 = pred[16,16,512]{2,1,0:T(8,128)(4,1)S(1)} reshape(pred[16,16,32,16]{3,2,1,0:T(8,128)(4,1)S(1)} %broadcast_in_dim.126) | data formatting | bytes 262144 | tf_op jit(solution)/shard_map/jit(_where)/broadcast_in_dim | solution.py:267
  111.5 3.6 %broadcast_in_dim.110 = pred[16,16,512]{2,1,0:T(8,128)(4,1)S(1)} reshape(pred[16,16,32,16]{3,2,1,0:T(8,128)(4,1)S(1)} %broadcast_in_dim.109) | data formatting | bytes 262144 | tf_op jit(solution)/shard_map/jit(_where)/broadcast_in_dim | solution.py:267
  115.1 36.3 %all-reduce.3.cloned.1.call-done = f32[24960]{0:T(1024)} async-done(((f32[24960]{0:T(1024)}), f32[24960]{0:T(1024)}) %all-reduce.3.cloned.1.call-update) | async-done | bytes 99856
  154.1 2.6 %broadcast_in_dim.118 = bf16[16,16,2,32,16]{4,3,1,2,0:T(8,128)(2,1)} broadcast(bf16[16,16,2,16]{3,1,2,0:T(8,128)(2,1)S(1)} %bitcast.56), dimensions={0,1,2,4} | broadcast | bytes 540672 | tf_op jit(solution)/shard_map/jit(_where)/broadcast_in_dim | solution.py:267
  156.6 7.8 %broadcast_in_dim.119 = bf16[16,16,2,512]{3,1,2,0:T(8,128)(2,1)S(1)} reshape(bf16[16,16,2,32,16]{4,3,1,2,0:T(8,128)(2,1)} %broadcast_in_dim.118) | data formatting | bytes 1048576 | tf_op jit(solution)/shard_map/jit(_where)/broadcast_in_dim | solution.py:267
  164.4 2.6 %broadcast_in_dim.124 = bf16[16,16,2,32,16]{4,3,1,2,0:T(8,128)(2,1)} broadcast(bf16[16,16,2,16]{3,1,2,0:T(8,128)(2,1)S(1)} %bitcast.57), dimensions={0,1,2,4} | broadcast | bytes 540672 | tf_op jit(solution)/shard_map/jit(_where)/broadcast_in_dim | solution.py:267
  167.0 7.8 %broadcast_in_dim.125 = bf16[16,16,2,512]{3,1,2,0:T(8,128)(2,1)S(1)} reshape(bf16[16,16,2,32,16]{4,3,1,2,0:T(8,128)(2,1)} %broadcast_in_dim.124) | data formatting | bytes 1048576 | tf_op jit(solution)/shard_map/jit(_where)/broadcast_in_dim | solution.py:267
  174.8 2.6 %broadcast_in_dim.130 = bf16[16,16,2,32,16]{4,3,1,2,0:T(8,128)(2,1)} broadcast(bf16[16,16,2,16]{3,1,2,0:T(8,128)(2,1)S(1)} %bitcast.58), dimensions={0,1,2,4} | broadcast | bytes 540672 | tf_op jit(solution)/shard_map/jit(_where)/broadcast_in_dim | solution.py:267
  177.3 7.8 %broadcast_in_dim.131 = bf16[16,16,2,512]{3,1,2,0:T(8,128)(2,1)S(1)} reshape(bf16[16,16,2,32,16]{4,3,1,2,0:T(8,128)(2,1)} %broadcast_in_dim.130) | data formatting | bytes 1048576 | tf_op jit(solution)/shard_map/jit(_where)/broadcast_in_dim | solution.py:267
  185.7 1.6 copy-done.1
  187.3 2.8 %power.1 = f32[16,16,128]{2,1,0:T(8,128)S(1)} custom-call(bf16[16,32,1024]{2,1,0:T(8,128)(2,1)S(1)} %maximum_maximum_fusion.w_ref, f32[16,16,1]{2,1,0:T(8,128)S(1)} %slice.94.quiet_ref, bf16[16,2,32,16,128]{4,3,2,1,0:T(8,128)(2,1)S(1)} %copy-done.1), custom_call_target="tpu_custom_call" | custom-call | tf_op jit(solution)/shard_map/power/pallas_call | solution.py:274
  192.8 5.2 %collective-permute-done.3 = f32[16,16,1]{2,1,0:T(8,128)S(1)} collective-permute-done((f32[16,16,1]{2,1,0:T(8,128)S(1)}, f32[16,16,1]{2,1,0:T(8,128)S(1)}, u32[]{:S(2)}, u32[]{:S(2)}) %collective-permute-start.3) | collective-permute-done | bytes 1056 | tf_op jit(solution)/shard_map/ppermute | solution.py:29
  198.2 1.5 collective-permute-start.4
  199.7 1.5 collective-permute-start.5
  201.2 1.6 collective-permute-done.4
  (77 shorter events, 18.1 us)
Async XLA Ops:
  6.5 5.7 %copy-start = (s32[64,16]{0,1:T(8,128)S(1)}, s32[64,16]{0,1:T(8,128)}, u32[]{:S(2)}) copy-start(s32[64,16]{0,1:T(8,128)} %param.8) | copy-start | bytes 12292
  6.5 28.8 %copy-start.2 = (bf16[2,64,32,128]{3,2,1,0:T(8,128)(2,1)S(1)}, bf16[2,64,32,128]{3,2,1,0:T(8,128)(2,1)}, u32[]{:S(2)}) copy-start(bf16[2,64,32,128]{3,2,1,0:T(8,128)(2,1)} %param.6) | copy-start | bytes 3145732
  6.5 5.8 %copy-start.4 = (f32[64,16]{0,1:T(8,128)S(1)}, f32[64,16]{0,1:T(8,128)}, u32[]{:S(2)}) copy-start(f32[64,16]{0,1:T(8,128)} %param.10) | copy-start | bytes 12292
  6.5 6.0 %copy-start.5 = (s32[64,16]{0,1:T(8,128)S(1)}, s32[64,16]{0,1:T(8,128)}, u32[]{:S(2)}) copy-start(s32[64,16]{0,1:T(8,128)} %param.9) | copy-start | bytes 12292
  6.5 6.1 %copy-start.7 = (s32[16,1]{0,1:T(1,128)S(1)}, s32[16,1]{0,1:T(1,128)}, u32[]{:S(2)}) copy-start(s32[16,1]{0,1:T(1,128)} %param.11) | copy-start | bytes 196
  6.5 6.2 %copy-start.6 = (s32[64]{0:T(128)S(1)}, s32[64]{0:T(128)}, u32[]{:S(2)}) copy-start(s32[64]{0:T(128)} %param.7) | copy-start | bytes 772
  6.6 80.9 %reduce-scatter.2.cloned.1.call-start = ((), (), s32[]{:S(2)}) async-start(), calls=%async_computation.1 | async-start | bytes 2654208 | tf_op jit(solution)/shard_map/reduce_scatter | solution.py:231
  8.0 16.7 %collective-permute-start = (bf16[2,32,32,128]{3,2,1,0:T(8,128)(2,1)S(1)}, bf16[2,32,32,128]{3,2,1,0:T(8,128)(2,1)S(1)}, u32[]{:S(2)}, u32[]{:S(2)}) collective-permute-start(bf16[2,32,32,128]{3,2,1,0:T(8,128)(2,1)S(1)} %get-tuple-element.11), channel_id=1, source_target_pairs={{0,8},{8,16},{16,24},{24,0},{1,9},{9,17},{17,25},{25,1},{2,10},{10... | collective-permute-start | bytes 1572872 | tf_op jit(solution)/shard_map/ppermute | solution.py:26
  11.0 24.4 %collective-permute-start.1 = (bf16[2,32,32,128]{3,2,1,0:T(8,128)(2,1)S(1)}, bf16[2,32,32,128]{3,2,1,0:T(8,128)(2,1)S(1)}, u32[]{:S(2)}, u32[]{:S(2)}) collective-permute-start(bf16[2,32,32,128]{3,2,1,0:T(8,128)(2,1)S(1)} %get-tuple-element.12), channel_id=1, source_target_pairs={{8,0},{16,8},{24,16},{0,24},{9,1},{17,9},{25,17},{1,25},{10,2},{18... | collective-permute-start | bytes 1572872 | tf_op jit(solution)/shard_map/ppermute | solution.py:29
  35.7 14.2 %copy-start.8 = (u32[32]{0:T(128)S(1)}, u32[32]{0:T(128)}, u32[]{:S(2)}) copy-start(u32[32]{0:T(128)} %constant.76) | copy-start | bytes 388
  49.9 101.5 %all-reduce.3.cloned.1.call-start = ((), (), s32[]{:S(2)}) async-start(), calls=%async_computation.2 | async-start | bytes 204800
  99.2 0.6 copy-start.3
  185.1 2.2 %copy-start.1 = (bf16[16,2,32,16,128]{4,3,2,1,0:T(8,128)(2,1)S(1)}, bf16[16,2,32,16,128]{4,3,2,1,0:T(8,128)(2,1)}, u32[]{:S(2)}) copy-start(bf16[16,2,32,16,128]{4,3,2,1,0:T(8,128)(2,1)} %get-tuple-element.8.v_ref) | copy-start | bytes 12582916
  190.2 2.6 %collective-permute-start.2 = (f32[16,16,1]{2,1,0:T(8,128)S(1)}, f32[16,16,1]{2,1,0:T(8,128)S(1)}, u32[]{:S(2)}, u32[]{:S(2)}) collective-permute-start(f32[16,16,1]{2,1,0:T(8,128)S(1)} %get-tuple-element.20), channel_id=1, source_target_pairs={{0,1},{1,2},{2,3},{3,4},{4,5},{5,6},{6,7},{8,9},{9,10},{10,11},{11... | collective-permute-start | bytes 3080 | tf_op jit(solution)/shard_map/ppermute | solution.py:26
  191.5 6.5 %collective-permute-start.3 = (f32[16,16,1]{2,1,0:T(8,128)S(1)}, f32[16,16,1]{2,1,0:T(8,128)S(1)}, u32[]{:S(2)}, u32[]{:S(2)}) collective-permute-start(f32[16,16,1]{2,1,0:T(8,128)S(1)} %get-tuple-element.21), channel_id=1, source_target_pairs={{1,0},{2,1},{3,2},{4,3},{5,4},{6,5},{7,6},{9,8},{10,9},{11,10},{12... | collective-permute-start | bytes 3080 | tf_op jit(solution)/shard_map/ppermute | solution.py:29
  198.2 4.6 %collective-permute-start.4 = (f32[1,16,128]{2,1,0:T(8,128)S(1)}, f32[1,16,128]{2,1,0:T(8,128)S(1)}, u32[]{:S(2)}, u32[]{:S(2)}) collective-permute-start(f32[1,16,128]{2,1,0:T(8,128)S(1)} %get-tuple-element.18), channel_id=1, source_target_pairs={{0,8},{8,16},{16,24},{24,0},{1,9},{9,17},{17,25},{25,1},{2,10},{10... | collective-permute-start | bytes 24584 | tf_op jit(solution)/shard_map/ppermute | solution.py:26
  199.7 3.7 %collective-permute-start.5 = (f32[1,16,128]{2,1,0:T(8,128)S(1)}, f32[1,16,128]{2,1,0:T(8,128)S(1)}, u32[]{:S(2)}, u32[]{:S(2)}) collective-permute-start(f32[1,16,128]{2,1,0:T(8,128)S(1)} %get-tuple-element.19), channel_id=1, source_target_pairs={{8,0},{16,8},{24,16},{0,24},{9,1},{17,9},{25,17},{1,25},{10,2},{18... | collective-permute-start | bytes 24584 | tf_op jit(solution)/shard_map/ppermute | solution.py:29
Sparse Core Ops, SparseCore 0:
  50.0 37.3 reduce-scatter.1
  100.0 51.2 all-reduce.2

commit v2 on v1

--- a/solution.py
+++ b/solution.py
@@ -14,21 +14,6 @@
 BLK = 128
 LOADING = 0.1
 VMEM_LIMIT = 48 << 20
-
-
-def with_halo(block, sides, width, periodic):
-    for axis, dim in sides:
-        count = lax.axis_size(axis)
-        forward = [(i, i + 1) for i in range(count - 1)]
-        if periodic:
-            forward.append((count - 1, 0))
-        backward = [(target, source) for source, target in forward]
-        low = lax.ppermute(
-            lax.slice_in_dim(block, block.shape[dim] - width, None, axis=dim), axis, forward
-        )
-        high = lax.ppermute(lax.slice_in_dim(block, 0, width, axis=dim), axis, backward)
-        block = jnp.concatenate([low, block, high], axis=dim)
-    return block
 
 
 def doppler_table(num_pulses):
@@ -154,13 +139,267 @@
     out_ref[2 * dof :, :] = jnp.broadcast_to(jnp.sum(xr[...], 0, keepdims=True), (8, lanes))
 
 
-def power_kernel(w_ref, quiet_ref, v_ref, out_ref):
-    num_chan = out_ref.shape[1]
-    flat = v_ref[0].reshape(w_ref.shape[2], v_ref.shape[4])
-    proj = jnp.dot(w_ref[0], flat, preferred_element_type=jnp.float32)
-    p0 = proj[:num_chan]
-    p1 = proj[num_chan:]
-    out_ref[0] = (p0 * p0 + p1 * p1) / quiet_ref[0]
+MESH = pl.DeviceIdType.MESH
+
+
+def scatter_kernel(n, g_ref, out_ref, pair, acc, right, left, psend, precv, rsend, rrecv, lsend, lrecv):
+    me = lax.axis_index("rng")
+    z = me // 2
+    c = me % 2
+    mate = 2 * z + 1 - c
+    ahead = lax.rem(me + 2, 2 * n)
+    behind = lax.rem(me + 2 * n - 2, 2 * n)
+    barrier = pltpu.get_barrier_semaphore()
+    pl.semaphore_signal(barrier, inc=1, device_id={"rng": mate}, device_id_type=MESH)
+    pl.semaphore_signal(barrier, inc=1, device_id={"rng": ahead}, device_id_type=MESH)
+    pl.semaphore_signal(barrier, inc=1, device_id={"rng": behind}, device_id_type=MESH)
+    pl.semaphore_wait(barrier, 3)
+
+    order = []
+    for t in range((n + 1) // 2):
+        order.append(n - 1 - t)
+        if t != n - 1 - t:
+            order.append(t)
+
+    def pair_copy(t):
+        return pltpu.make_async_remote_copy(
+            src_ref=g_ref.at[2 * t + 1 - c],
+            dst_ref=pair.at[t],
+            send_sem=psend.at[t],
+            recv_sem=precv.at[t],
+            device_id={"rng": mate},
+            device_id_type=MESH,
+        )
+
+    def right_copy(t):
+        return pltpu.make_async_remote_copy(
+            src_ref=acc.at[t],
+            dst_ref=right.at[t],
+            send_sem=rsend.at[t],
+            recv_sem=rrecv.at[t],
+            device_id={"rng": ahead},
+            device_id_type=MESH,
+        )
+
+    def left_copy(t):
+        return pltpu.make_async_remote_copy(
+            src_ref=acc.at[t],
+            dst_ref=left.at[t],
+            send_sem=lsend.at[t],
+            recv_sem=lrecv.at[t],
+            device_id={"rng": behind},
+            device_id_type=MESH,
+        )
+
+    for t in order:
+        pair_copy(t).start()
+    for t in order:
+        pair_copy(t).wait_recv()
+        acc[t] = g_ref[2 * t + c] + pair[t]
+
+        @pl.when(jnp.logical_and(z == 0, t > 0))
+        def _(t=t):
+            right_copy(t).start()
+
+        @pl.when(jnp.logical_and(z == n - 1, t < n - 1))
+        def _(t=t):
+            left_copy(t).start()
+
+    for s in range(n - 1):
+        t = n - 1 - s
+
+        @pl.when(jnp.logical_and(z > 0, z < t))
+        def _(t=t):
+            right_copy(t).wait_recv()
+            acc[t] = acc[t] + right[t]
+            right_copy(t).start()
+
+        @pl.when(jnp.logical_and(z < n - 1, z > s))
+        def _(t=s):
+            left_copy(t).wait_recv()
+            acc[t] = acc[t] + left[t]
+            left_copy(t).start()
+
+    for t in range(n):
+
+        @pl.when(z == t)
+        def _(t=t):
+            total = acc[t]
+            if t > 0:
+                right_copy(t).wait_recv()
+                total = total + right[t]
+            if t < n - 1:
+                left_copy(t).wait_recv()
+                total = total + left[t]
+            out_ref[...] = total
+
+    for t in range(n):
+        pair_copy(t).wait_send()
+
+        @pl.when(z < t)
+        def _(t=t):
+            right_copy(t).wait_send()
+
+        @pl.when(z > t)
+        def _(t=t):
+            left_copy(t).wait_send()
+
+
+def apply_kernel(
+    halves,
+    per,
+    dof,
+    pay_ref,
+    bins_ref,
+    *refs,
+):
+    v_refs = refs[:halves]
+    (out_ref, v_all, gat, expand, power, edge, halo, sums, az_lo, az_hi) = refs[halves : halves + 10]
+    (vsem, gsend, grecv, esend, erecv, asend, arecv) = refs[halves + 10 :]
+    me = lax.axis_index("rng")
+    az = lax.axis_index("az")
+    n = lax.axis_size("rng")
+    m = lax.axis_size("az")
+    beams, num_chan, cells = out_ref.shape
+    pulses, num_sel = v_all.shape[2], v_all.shape[3]
+    taps = pulses * num_sel
+    az_next = lax.rem(az + 1, m)
+    az_prev = lax.rem(az + m - 1, m)
+    barrier = pltpu.get_barrier_semaphore()
+    for d in range(1, n):
+        peer = lax.rem(me + d, n)
+        pl.semaphore_signal(barrier, inc=1, device_id={"rng": peer}, device_id_type=MESH)
+    for other in (az_next, az_prev):
+        pl.semaphore_signal(barrier, inc=1, device_id={"az": other}, device_id_type=MESH)
+    share = beams // halves
+    loads = []
+    for h in range(halves):
+        load = pltpu.make_async_copy(v_refs[h], v_all.at[pl.ds(h * share, share)], vsem.at[h])
+        load.start()
+        loads.append(load)
+    pl.semaphore_wait(barrier, n + 1)
+
+    copies = []
+    for d in range(1, n):
+        peer = lax.rem(me + d, n)
+        copy = pltpu.make_async_remote_copy(
+            src_ref=pay_ref,
+            dst_ref=gat.at[me],
+            send_sem=gsend.at[d],
+            recv_sem=grecv.at[d],
+            device_id={"rng": peer},
+            device_id_type=MESH,
+        )
+        copy.start()
+        copies.append(copy)
+    gat[me] = pay_ref[...]
+    depth = expand.shape[1]
+    wide = expand.shape[2]
+    src = lax.broadcasted_iota(jnp.int32, (depth, wide), 0)
+    dst = lax.broadcasted_iota(jnp.int32, (depth, wide), 1)
+    want = (dst // taps) * num_sel + dst % num_sel
+    expand[0] = (src == want).astype(jnp.float32).astype(jnp.bfloat16)
+    expand[1] = (src == want + dof).astype(jnp.float32).astype(jnp.bfloat16)
+    for load in loads:
+        load.wait()
+    for copy in copies:
+        copy.wait_recv()
+    rows = gat.shape[1] - beams
+    count = jnp.zeros((beams, gat.shape[2]), jnp.float32)
+    for r in range(n):
+        count = count + gat[r, rows:, :]
+    sums[0] = jnp.zeros(sums.shape[1:], jnp.float32)
+    for b in range(beams):
+        sums[b, :1, :] = count[b : b + 1]
+    freq = lax.broadcasted_iota(jnp.int32, (num_chan, taps), 1) // num_sel
+
+    def one(b, carry):
+        if per >= num_chan:
+            ratio = per // num_chan
+            start = pl.multiple_of((b % ratio) * num_chan, 8)
+            w = gat[b // ratio, pl.ds(start, num_chan), :]
+        else:
+            split = num_chan // per
+            w = jnp.concatenate([gat[b * split + t, :per, :] for t in range(split)], 0)
+        w = w * sums[b, :1, :]
+        quiet = w[:, 2 * dof : 2 * dof + 1]
+        wb = w.astype(jnp.bfloat16)
+        centre = bins_ref[b]
+        planes = []
+        for part in range(2):
+            spread = jnp.dot(wb, expand[part], preferred_element_type=jnp.float32)
+            plane = jnp.zeros((num_chan, taps), jnp.float32)
+            for q in range(BINS):
+                f = lax.rem(centre + (q - BINS // 2 + pulses), pulses)
+                plane = jnp.where(freq == f, spread[:, q * taps : (q + 1) * taps], plane)
+            planes.append(plane)
+        top = jnp.concatenate([planes[0], planes[1]], 1)
+        low = jnp.concatenate([-planes[1], planes[0]], 1)
+        lhs = jnp.concatenate([top, low], 0).astype(jnp.bfloat16)
+        flat = v_all[b].reshape(2 * taps, cells)
+        proj = jnp.dot(lhs, flat, preferred_element_type=jnp.float32)
+        p0 = proj[:num_chan]
+        p1 = proj[num_chan:]
+        power[b] = (p0 * p0 + p1 * p1) / quiet
+        return carry
+
+    lax.fori_loop(0, beams, one, 0)
+    items = beams * num_chan
+    turned = power[...].reshape(items, cells).T
+    edge[0] = turned[:8]
+    edge[1] = turned[cells - 8 :]
+
+    def edge_copy(side):
+        target = lax.rem(me + 1, n) if side else lax.rem(me + n - 1, n)
+        return pltpu.make_async_remote_copy(
+            src_ref=edge.at[side],
+            dst_ref=halo.at[side],
+            send_sem=esend.at[side],
+            recv_sem=erecv.at[side],
+            device_id={"rng": target},
+            device_id_type=MESH,
+        )
+
+    for side in range(2):
+        edge_copy(side).start()
+    for side in range(2):
+        edge_copy(side).wait()
+    before = jnp.where(me > 0, halo[1, 7:8], 0.0)
+    after = jnp.where(me < n - 1, halo[0, 0:1], 0.0)
+    turned = (
+        jnp.concatenate([before, turned[:-1]], 0)
+        + turned
+        + jnp.concatenate([turned[1:], after], 0)
+    )
+    sums[...] = turned.T.reshape(beams, num_chan, cells)
+    up = pltpu.make_async_remote_copy(
+        src_ref=sums.at[beams - 1],
+        dst_ref=az_lo,
+        send_sem=asend.at[0],
+        recv_sem=arecv.at[0],
+        device_id={"az": az_next},
+        device_id_type=MESH,
+    )
+    down = pltpu.make_async_remote_copy(
+        src_ref=sums.at[0],
+        dst_ref=az_hi,
+        send_sem=asend.at[1],
+        recv_sem=arecv.at[1],
+        device_id={"az": az_prev},
+        device_id_type=MESH,
+    )
+    up.start()
+    down.start()
+    for b in range(1, beams - 1):
+        out_ref[b] = (sums[b - 1] + sums[b] + sums[b + 1]) / 9.0
+    up.wait_recv()
+    down.wait_recv()
+    out_ref[0] = (az_lo[...] + sums[0] + sums[1]) / 9.0
+    out_ref[beams - 1] = (sums[beams - 2] + sums[beams - 1] + az_hi[...]) / 9.0
+    up.wait_send()
+    down.wait_send()
+    for copy in copies:
+        copy.wait_send()
 
 
 def body(echoes, arc_start, arc_offsets, doppler_bins, steer_angles, train_mask):
@@ -183,7 +422,6 @@
     def own(x):
         return lax.dynamic_slice_in_dim(x, cycle_pos * beam_count, beam_count, axis=0)
 
-    extended = with_halo(echoes, (("az", 1),), ARC // 2, True)
     arc_first = (own(arc_start) - cycle_pos * columns + ARC // 2) % COLS
     col_index = arc_first[:, None] + own(arc_offsets)
     bins_own = own(doppler_bins)
@@ -195,30 +433,60 @@
         .astype(jnp.bfloat16)
     )
     smem = pl.BlockSpec(memory_space=pltpu.SMEM)
-    ext_cols = extended.shape[1]
-    v_all, gram = pl.pallas_call(
-        snap_gram_kernel,
-        grid=(beam_count,),
-        in_specs=[
-            smem,
-            smem,
-            smem,
-            smem,
-            pl.BlockSpec((2, ext_cols, num_pulses, cells), lambda b: (0, 0, 0, 0)),
-            pl.BlockSpec(table.shape, lambda b: (0, 0)),
-            pl.BlockSpec((1, 1, cells), lambda b: (b, 0, 0)),
-        ],
-        out_specs=[
-            pl.BlockSpec((1, 2, num_pulses, num_sel, cells), lambda b: (b, 0, 0, 0, 0)),
-            pl.BlockSpec((1, dof, chan_count * dof), lambda b: (b, 0, 0)),
-        ],
-        out_shape=[
-            jax.ShapeDtypeStruct((beam_count, 2, num_pulses, num_sel, cells), jnp.bfloat16),
-            jax.ShapeDtypeStruct((beam_count, dof, chan_count * dof), jnp.float32),
-        ],
-        compiler_params=pltpu.CompilerParams(vmem_limit_bytes=VMEM_LIMIT),
-        name="snap_gram",
-    )(col_index, bins_own, jnp.cos(angles), jnp.sin(angles), extended, table, cell_mask)
+
+    def snap_gram(extended, first, last, base):
+        share = last - first
+        ext_cols = extended.shape[1]
+        return pl.pallas_call(
+            snap_gram_kernel,
+            grid=(share,),
+            in_specs=[
+                smem,
+                smem,
+                smem,
+                smem,
+                pl.BlockSpec((2, ext_cols, num_pulses, cells), lambda b: (0, 0, 0, 0)),
+                pl.BlockSpec(table.shape, lambda b: (0, 0)),
+                pl.BlockSpec((1, 1, cells), lambda b: (b, 0, 0)),
+            ],
+            out_specs=[
+                pl.BlockSpec((1, 2, num_pulses, num_sel, cells), lambda b: (b, 0, 0, 0, 0)),
+                pl.BlockSpec((1, dof, chan_count * dof), lambda b: (b, 0, 0)),
+            ],
+            out_shape=[
+                jax.ShapeDtypeStruct((share, 2, num_pulses, num_sel, cells), jnp.bfloat16),
+                jax.ShapeDtypeStruct((share, dof, chan_count * dof), jnp.float32),
+            ],
+            compiler_params=pltpu.CompilerParams(vmem_limit_bytes=VMEM_LIMIT),
+            cost_estimate=pl.CostEstimate(
+                flops=share * 600_000_000, bytes_accessed=share * 1_500_000, transcendentals=0
+            ),
+            name="snap_gram",
+        )(
+            col_index[first:last] - base,
+            bins_own[first:last],
+            jnp.cos(angles)[first:last],
+            jnp.sin(angles)[first:last],
+            extended,
+            table,
+            cell_mask[first:last],
+        )
+
+    width = ARC // 2
+    forward = [(i, (i + 1) % cycle_size) for i in range(cycle_size)]
+    backward = [(target, source) for source, target in forward]
+    low = lax.ppermute(echoes[:, columns - width :], "az", forward)
+    high = lax.ppermute(echoes[:, :width], "az", backward)
+    step = COLS // BEAMS
+    half = beam_count // 2
+    if (half - 1) * step + step - 1 + ARC - 1 < width + columns and half * step >= width:
+        v_lo, gram_lo = snap_gram(jnp.concatenate([low, echoes], 1), 0, half, 0)
+        v_hi, gram_hi = snap_gram(jnp.concatenate([echoes, high], 1), half, beam_count, width)
+        v_parts = (v_lo, v_hi)
+        gram = jnp.concatenate([gram_lo, gram_hi], 0)
+    else:
+        v_one, gram = snap_gram(jnp.concatenate([low, echoes, high], 1), 0, beam_count, 0)
+        v_parts = (v_one,)
 
     per = item_count // rng_size
     if per < chan_count:
@@ -228,7 +496,21 @@
         width = per
     else:
         width = chan_count
-    part = lax.psum_scatter(gram, "rng", scatter_dimension=0, tiled=True)
+    vm = pltpu.VMEM
+    dma = pltpu.SemaphoreType.DMA
+    line = rng_size // 2
+    chunk = (gram.shape[0] // rng_size, dof, gram.shape[2])
+    part = pl.pallas_call(
+        functools.partial(scatter_kernel, line),
+        in_specs=[pl.BlockSpec(memory_space=vm)],
+        out_specs=pl.BlockSpec(memory_space=vm),
+        out_shape=jax.ShapeDtypeStruct(chunk, jnp.float32),
+        scratch_shapes=[vm((line,) + chunk, jnp.float32)] * 4 + [dma((line,))] * 6,
+        compiler_params=pltpu.CompilerParams(
+            collective_id=0, has_side_effects=True, vmem_limit_bytes=VMEM_LIMIT
+        ),
+        name="scatter",
+    )(gram.reshape((rng_size,) + chunk))
     lead = part.shape[0]
     mats = part.reshape(lead, dof, width, dof).transpose(1, 3, 0, 2).reshape(dof, dof, per)
     flip = jnp.swapaxes(mats, 0, 1)
@@ -236,7 +518,6 @@
     row, col = ids[:, None, None], ids[None, :, None]
     h_re = jnp.where(row >= col, mats, flip)
     h_im = jnp.where(row < col, mats, jnp.where(row > col, -flip, 0.0))
-    vm = pltpu.VMEM
     solved = pl.pallas_call(
         solve_kernel,
         out_shape=jax.ShapeDtypeStruct((2 * dof + 8, per), jnp.float32),
@@ -249,45 +530,49 @@
         compiler_params=pltpu.CompilerParams(vmem_limit_bytes=VMEM_LIMIT),
         name="solve",
     )(h_re, h_im)
-    body_size = (2 * dof + 1) * per
+    lanes = 128
     local_count = (BLK * jnp.sum(train_mask, axis=1)).astype(jnp.float32)
-    payload = jnp.concatenate([solved[: 2 * dof + 1].reshape(body_size), local_count])
-    gathered = lax.all_gather(payload, "rng", axis=0)
-    count = jnp.sum(gathered[:, body_size:], axis=0)
-    sol = gathered[:, :body_size].reshape(rng_size, 2 * dof + 1, per)
-    sol = jnp.swapaxes(sol, 1, 2).reshape(beam_count, chan_count, 2 * dof + 1)
-    sol = sol * count[:, None, None]
-    quiet = sol[:, :, 2 * dof :]
-    adapted = sol[:, :, : 2 * dof].astype(jnp.bfloat16)
-    adapted = adapted.reshape(beam_count, chan_count, 2, BINS, 1, num_sel)
-    freq = jnp.arange(num_pulses, dtype=jnp.int32)
-    spread = jnp.zeros((beam_count, chan_count, 2, num_pulses, num_sel), jnp.bfloat16)
-    for q in range(BINS):
-        hit = ((bins_own + (q - BINS // 2)) % num_pulses)[:, :, None] == freq
-        spread = jnp.where(hit[:, :, None, :, None], adapted[:, :, :, q], spread)
+    pad_rows = -per % 8
+    payload = jnp.concatenate(
+        [
+            jnp.pad(solved.T, ((0, pad_rows), (0, lanes - solved.shape[0]))),
+            jnp.broadcast_to(local_count[:, None], (beam_count, lanes)),
+        ],
+        0,
+    )
+    halves = len(v_parts)
+    any_spec = pl.BlockSpec(memory_space=pl.ANY)
     taps = num_pulses * num_sel
-    spread = spread.reshape(beam_count, chan_count, 2, taps)
-    w_re, w_im = spread[:, :, 0], spread[:, :, 1]
-    weights = jnp.concatenate(
-        [jnp.concatenate([w_re, w_im], 2), jnp.concatenate([-w_im, w_re], 2)], 1
-    )
-    power_map = pl.pallas_call(
-        power_kernel,
-        grid=(beam_count,),
-        in_specs=[
-            pl.BlockSpec((1, 2 * chan_count, 2 * taps), lambda b: (b, 0, 0)),
-            pl.BlockSpec((1, chan_count, 1), lambda b: (b, 0, 0)),
-            pl.BlockSpec((1, 2, num_pulses, num_sel, cells), lambda b: (b, 0, 0, 0, 0)),
+    block = (chan_count, cells)
+    out = pl.pallas_call(
+        functools.partial(apply_kernel, halves, per, dof),
+        in_specs=[pl.BlockSpec(memory_space=vm)] * 2 + [any_spec] * halves,
+        out_specs=pl.BlockSpec(memory_space=vm),
+        out_shape=jax.ShapeDtypeStruct((beam_count,) + block, jnp.float32),
+        scratch_shapes=[
+            vm((beam_count, 2, num_pulses, num_sel, cells), jnp.bfloat16),
+            vm((rng_size,) + payload.shape, jnp.float32),
+            vm((2, lanes, BINS * taps), jnp.bfloat16),
+            vm((beam_count,) + block, jnp.float32),
+            vm((2, 8, item_count), jnp.float32),
+            vm((2, 8, item_count), jnp.float32),
+            vm((beam_count,) + block, jnp.float32),
+            vm(block, jnp.float32),
+            vm(block, jnp.float32),
+            dma((halves,)),
+            dma((rng_size,)),
+            dma((rng_size,)),
+            dma((2,)),
+            dma((2,)),
+            dma((2,)),
+            dma((2,)),
         ],
-        out_specs=pl.BlockSpec((1, chan_count, cells), lambda b: (b, 0, 0)),
-        out_shape=jax.ShapeDtypeStruct((beam_count, chan_count, cells), jnp.float32),
-        compiler_params=pltpu.CompilerParams(vmem_limit_bytes=VMEM_LIMIT),
-        name="power",
-    )(weights, quiet, v_all)
-    range_ext = with_halo(power_map, (("rng", 2),), 1, False)
-    row_sums = range_ext[:, :, :-2] + range_ext[:, :, 1:-1] + range_ext[:, :, 2:]
-    beam_ext = with_halo(row_sums, (("az", 0),), 1, True)
-    return (beam_ext[:-2] + beam_ext[1:-1] + beam_ext[2:]) / 9.0
+        compiler_params=pltpu.CompilerParams(
+            collective_id=1, has_side_effects=True, vmem_limit_bytes=VMEM_LIMIT
+        ),
+        name="apply",
+    )(payload, bins_own[:, :, None], *v_parts)
+    return out
 
 
 def solution(mesh):

time: 213 us -> 119 us (0.56); the launches traced: 211 us -> 119 us
  waiting for transfers between devices: 102 us -> 22.1 us
  Pallas kernels: 24.5 us -> 77.3 us
  local copies, waits for them, and re-layouts: 56 us -> 11.4 us
  between operations: 14.5 us -> 0.16 us
  starting transfers between devices: 9.69 us -> 4.05 us
    pallas_call x2 -> x4, Pallas kernels: 16.9 us -> 69.7 us  [the longest x1 36.1 us: body(): pl.pallas_call(functools.partial(scatter_kernel, line), in_specs=[pl.Bloc...]
    broadcast_in_dim x12 -> x1, local copies, waits for them, and re-layouts: 46 us -> 0.17 us  [body(): bins_own[:, :, None]]
    unnamed x3 -> x0, waiting for transfers between devices: 36.3 us -> none
    reduce_scatter x1 -> x0, waiting for transfers between devices: 36.1 us -> none  [body(): part = lax.psum_scatter(gram, 'rng', scatter_dimension=0, tiled=True)]
    ppermute x6 -> x2, waiting for transfers between devices: 29.8 us -> 22.1 us  [the longest x1 11.5 us: body(): low = lax.ppermute(echoes[:, columns - width:], 'az', forward)]
    ppermute x6 -> x2, starting transfers between devices: 9.61 us -> 4.05 us  [the longest x1 3.03 us: body(): low = lax.ppermute(echoes[:, columns - width:], 'az', forward)]
    reshape x4, local copies, waits for them, and re-layouts: 2.41 us -> 5.46 us  [body(): part.reshape(lead, dof, width, dof).transpose(1, 3, 0, 2)]
  transfers between devices with their start and end apart: 8 -> 2, of which waited for: 7 -> 2; matrix products, arithmetic and copies ran while one was open for 8% -> 1% of each run, Pallas kernels for 0% -> 0%
where the time goes in v2:
time: 119 us
  Pallas kernels  77.3 us (65%)
  waiting for transfers between devices  22.1 us (19%)
  local copies, waits for them, and re-layouts  11.4 us (10%)
  other arithmetic  4.08 us (3%)
  starting transfers between devices  4.05 us (3%)
    pallas_call x1, Pallas kernels, body(): pl.pallas_call(functools.partial(scatter_kernel, line), in_specs=[pl.Bloc...  36.1 us
    pallas_call x1, Pallas kernels, body(): pl.pallas_call(functools.partial(apply_kernel, halves, per, dof), in_spec...  19.8 us
    pallas_call x2, Pallas kernels, snap_gram(): pl.pallas_call(snap_gram_kernel, grid=(share,), in_specs=[smem, smem, sme...  13.9 us
    ppermute x1, waiting for transfers between devices, body(): low = lax.ppermute(echoes[:, columns - width:], 'az', forward)  11.5 us
    ppermute x1, waiting for transfers between devices, body(): high = lax.ppermute(echoes[:, :width], 'az', backward)  10.6 us
    pallas_call x1, Pallas kernels, body(): pl.pallas_call(solve_kernel, out_shape=jax.ShapeDtypeStruct((2 * dof + 8,...  7.55 us
    reshape x4, local copies, waits for them, and re-layouts, body(): part.reshape(lead, dof, width, dof).transpose(1, 3, 0, 2)  5.46 us
    unnamed x20, local copies, waits for them, and re-layouts  3.83 us
  transfers between devices with their start and end apart: 2, of which 2 were waited for; matrix products, arithmetic and copies ran while one was open for 1% of the time, Pallas kernels for 0%

profile of v2, /device:TPU:0, one launch (start us, length us, event | category | flops | bytes accessed | tf_op | source)
XLA Modules:
  0.0 119.1 jit_solution(4612037519857313061)
XLA Ops:
  0.0 1.4 %fusion.10 = (bf16[2,32,32,128]{3,2,1,0:T(8,128)(2,1)S(1)}, bf16[2,32,32,128]{3,2,1,0:T(8,128)(2,1)S(1)}) fusion(bf16[2,64,32,128]{3,2,1,0:T(8,128)(2,1)} %param.6), kind=kLoop, calls=%fused_computation.37 | loop fusion | bytes 2097152 | tf_op jit(solution)/shard_map/slice | solution.py:478
  1.4 3.0 %collective-permute-start = (bf16[2,32,32,128]{3,2,1,0:T(8,128)(2,1)S(1)}, bf16[2,32,32,128]{3,2,1,0:T(8,128)(2,1)S(1)}, u32[]{:S(2)}, u32[]{:S(2)}) collective-permute-start(bf16[2,32,32,128]{3,2,1,0:T(8,128)(2,1)S(1)} %get-tuple-element.17), channel_id=1, source_target_pairs={{0,8},{8,16},{16,24},{24,0},{1,9},{9,17},{17,25},{25,1},{2,10},{10... | collective-permute-start | bytes 1572872 | tf_op jit(solution)/shard_map/ppermute | solution.py:478
  4.4 1.0 collective-permute-start.1
  5.5 0.1 sine_convert_fusion
  5.5 0.1 fusion.8
  6.0 0.1 and_select_fusion
  6.3 0.2 copy.21.bins_ref
  6.7 11.5 %collective-permute-done = bf16[2,32,32,128]{3,2,1,0:T(8,128)(2,1)S(1)} collective-permute-done((bf16[2,32,32,128]{3,2,1,0:T(8,128)(2,1)S(1)}, bf16[2,32,32,128]{3,2,1,0:T(8,128)(2,1)S(1)}, u32[]{:S(2)}, u32[]{:S(2)}) %collective-permute-start) | collective-permute-done | bytes 524320 | tf_op jit(solution)/shard_map/ppermute | solution.py:478
  18.2 10.6 %collective-permute-done.1 = bf16[2,32,32,128]{3,2,1,0:T(8,128)(2,1)S(1)} collective-permute-done((bf16[2,32,32,128]{3,2,1,0:T(8,128)(2,1)S(1)}, bf16[2,32,32,128]{3,2,1,0:T(8,128)(2,1)S(1)}, u32[]{:S(2)}, u32[]{:S(2)}) %collective-permute-start.1) | collective-permute-done | bytes 524320 | tf_op jit(solution)/shard_map/ppermute | solution.py:479
  28.8 0.3 pad_maximum_fusion.1
  29.1 6.9 %snap_gram.2 = (bf16[8,2,32,16,128]{4,3,2,1,0:T(8,128)(2,1)S(1)}, f32[8,48,768]{2,1,0:T(8,128)S(1)}) custom-call(s32[8,16]{1,0:T(8,128)S(1)} %get-tuple-element.25.col_ref, s32[8,16]{1,0:T(8,128)S(1)} %get-tuple-element.23.bins_ref, f32[8,16]{1,0:T(8,128)S(1)} %get-tuple-element.36.cos_ref, f32[8,16]{1,0:T(8,128)S(1)} %get-tuple-element.19.sin_ref, ...), custom_call_target="tpu_custom_call" | custom-call | flops 4800000000 | bytes 12000000 | tf_op jit(solution)/shard_map/snap_gram/pallas_call | solution.py:440
  36.2 6.9 %snap_gram.3 = (bf16[8,2,32,16,128]{4,3,2,1,0:T(8,128)(2,1)S(1)}, f32[8,48,768]{2,1,0:T(8,128)S(1)}) custom-call(s32[8,16]{1,0:T(8,128)S(1)} %get-tuple-element.26.col_ref, s32[8,16]{1,0:T(8,128)S(1)} %get-tuple-element.24.bins_ref, f32[8,16]{1,0:T(8,128)S(1)} %get-tuple-element.35.cos_ref, f32[8,16]{1,0:T(8,128)S(1)} %get-tuple-element.20.sin_ref, ...), custom_call_target="tpu_custom_call" | custom-call | flops 4800000000 | bytes 12000000 | tf_op jit(solution)/shard_map/snap_gram/pallas_call | solution.py:440
  43.1 1.3 %copy-done.1 = bf16[8,2,32,16,128]{4,3,2,1,0:T(8,128)(2,1)} copy-done((bf16[8,2,32,16,128]{4,3,2,1,0:T(8,128)(2,1)}, bf16[8,2,32,16,128]{4,3,2,1,0:T(8,128)(2,1)S(1)}, u32[]{:S(2)}) %copy-start.1) | copy-done | bytes 2097176
  44.4 0.2 pad_maximum_fusion
  44.6 36.1 %scatter.1 = f32[2,48,768]{2,1,0:T(8,128)S(1)} custom-call(f32[8,2,48,768]{3,2,1,0:T(8,128)S(1)} %bitcast.19), custom_call_target="tpu_custom_call" | custom-call | tf_op jit(solution)/shard_map/scatter/pallas_call | solution.py:503
  80.7 1.3 %reshape.65 = f32[2,48,16,48]{3,2,1,0:T(8,128)} reshape(f32[2,48,768]{2,1,0:T(8,128)S(1)} %scatter.1) | data formatting | bytes 589824 | tf_op jit(solution)/shard_map/reshape | solution.py:515
  82.0 1.2 %copy.16 = f32[2,48,16,48]{3,2,0,1:T(8,128)S(1)} copy(f32[2,48,16,48]{3,2,1,0:T(8,128)} %reshape.65) | data formatting | bytes 589824 | tf_op jit(solution)/shard_map/reshape | solution.py:515
  83.2 1.5 %copy.17 = f32[48,48,32]{2,0,1:T(8,128)} copy(f32[48,48,32]{1,2,0:T(8,128)S(1)} %bitcast.20) | data formatting | bytes 589824 | tf_op jit(solution)/shard_map/reshape | solution.py:515
  84.7 1.4 %copy.18 = f32[48,48,32]{2,1,0:T(8,128)} copy(f32[48,48,32]{1,2,0:T(8,128)S(1)} %bitcast.21) | data formatting | bytes 589824 | tf_op jit(solution)/shard_map/reshape | solution.py:515
  86.2 3.1 %fusion.1 = (f32[48,48,32]{2,1,0:T(8,128)S(1)}, f32[48,48,32]{2,1,0:T(8,128)S(1)}) fusion(f32[48,48,32]{2,1,0:T(8,128)} %copy.18, f32[48,48,32]{2,0,1:T(8,128)} %copy.17, pred[48,48]{1,0:T(8,128)(4,1)S(1)} %get-tuple-element.39, pred[48,48]{1,0:T(8,128)(4,1)S(1)} %get-tuple-element.40, pred[48,48]{1,0:T(8,128)(4,1)S(1)} %iota_compare_fusion.3), kind=kLoop, calls=%fused_computation.6 | loop fusion | flops 294912 | bytes 1186560 | tf_op jit(solution)/shard_map/jit(_where)/select_n | solution.py:520
  89.3 7.5 %solve.1 = f32[104,32]{1,0:T(8,128)S(1)} custom-call(f32[48,48,32]{2,1,0:T(8,128)S(1)} %get-tuple-element.14.hr_in, f32[48,48,32]{2,1,0:T(8,128)S(1)} %get-tuple-element.13.hi_in), custom_call_target="tpu_custom_call" | custom-call | tf_op jit(solution)/shard_map/solve/pallas_call | solution.py:521
  97.0 1.6 %copy-done.2 = bf16[8,2,32,16,128]{4,3,2,1,0:T(8,128)(2,1)S(1)} copy-done((bf16[8,2,32,16,128]{4,3,2,1,0:T(8,128)(2,1)S(1)}, bf16[8,2,32,16,128]{4,3,2,1,0:T(8,128)(2,1)}, u32[]{:S(2)}) %copy-start.2) | copy-done | bytes 2097176
  98.6 19.8 %apply.1 = f32[16,16,128]{2,1,0:T(8,128)S(1)} custom-call(f32[48,128]{1,0:T(8,128)S(1)} %select_maximum_fusion.pay_ref, s32[16,16,1]{2,1,0:T(8,128)S(1)} %copy.21.bins_ref, bf16[8,2,32,16,128]{4,3,2,1,0:T(8,128)(2,1)S(1)} %get-tuple-element.11.refs_0_, bf16[8,2,32,16,128]{4,3,2,1,0:T(8,128)(2,1)S(1)} %copy-done.2), custom_call_target="tpu_custom_call" | custom-call | tf_op jit(solution)/shard_map/apply/pallas_call | solution.py:547
  118.4 0.7 copy.26
  (34 shorter events, 1.1 us)
Async XLA Ops:
  0.0 5.7 %copy-start = (f32[64,16]{0,1:T(8,128)S(1)}, f32[64,16]{0,1:T(8,128)}, u32[]{:S(2)}) copy-start(f32[64,16]{0,1:T(8,128)} %param.10) | copy-start | bytes 12292
  0.0 28.8 %copy-start.3 = (bf16[2,64,32,128]{3,2,1,0:T(8,128)(2,1)S(1)}, bf16[2,64,32,128]{3,2,1,0:T(8,128)(2,1)}, u32[]{:S(2)}) copy-start(bf16[2,64,32,128]{3,2,1,0:T(8,128)(2,1)} %param.6) | copy-start | bytes 3145732
  0.0 5.8 %copy-start.5 = (s32[64,16]{0,1:T(8,128)S(1)}, s32[64,16]{0,1:T(8,128)}, u32[]{:S(2)}) copy-start(s32[64,16]{0,1:T(8,128)} %param.8) | copy-start | bytes 12292
  0.0 5.8 %copy-start.4 = (s32[64,16]{0,1:T(8,128)S(1)}, s32[64,16]{0,1:T(8,128)}, u32[]{:S(2)}) copy-start(s32[64,16]{0,1:T(8,128)} %param.9) | copy-start | bytes 12292
  0.0 6.0 %copy-start.6 = (s32[64]{0:T(128)S(1)}, s32[64]{0:T(128)}, u32[]{:S(2)}) copy-start(s32[64]{0:T(128)} %param.7) | copy-start | bytes 772
  0.0 6.2 %copy-start.7 = (s32[16,1]{0,1:T(1,128)S(1)}, s32[16,1]{0,1:T(1,128)}, u32[]{:S(2)}) copy-start(s32[16,1]{0,1:T(1,128)} %param.11) | copy-start | bytes 196
  1.4 16.8 %collective-permute-start = (bf16[2,32,32,128]{3,2,1,0:T(8,128)(2,1)S(1)}, bf16[2,32,32,128]{3,2,1,0:T(8,128)(2,1)S(1)}, u32[]{:S(2)}, u32[]{:S(2)}) collective-permute-start(bf16[2,32,32,128]{3,2,1,0:T(8,128)(2,1)S(1)} %get-tuple-element.17), channel_id=1, source_target_pairs={{0,8},{8,16},{16,24},{24,0},{1,9},{9,17},{17,25},{25,1},{2,10},{10... | collective-permute-start | bytes 1572872 | tf_op jit(solution)/shard_map/ppermute | solution.py:478
  4.4 24.4 %collective-permute-start.1 = (bf16[2,32,32,128]{3,2,1,0:T(8,128)(2,1)S(1)}, bf16[2,32,32,128]{3,2,1,0:T(8,128)(2,1)S(1)}, u32[]{:S(2)}, u32[]{:S(2)}) collective-permute-start(bf16[2,32,32,128]{3,2,1,0:T(8,128)(2,1)S(1)} %get-tuple-element.18), channel_id=1, source_target_pairs={{8,0},{16,8},{24,16},{0,24},{9,1},{17,9},{25,17},{1,25},{10,2},{18... | collective-permute-start | bytes 1572872 | tf_op jit(solution)/shard_map/ppermute | solution.py:479
  43.1 1.3 %copy-start.1 = (bf16[8,2,32,16,128]{4,3,2,1,0:T(8,128)(2,1)}, bf16[8,2,32,16,128]{4,3,2,1,0:T(8,128)(2,1)S(1)}, u32[]{:S(2)}) copy-start(bf16[8,2,32,16,128]{4,3,2,1,0:T(8,128)(2,1)S(1)} %get-tuple-element.12.refs_1_) | copy-start | bytes 6291460
  97.0 1.6 %copy-start.2 = (bf16[8,2,32,16,128]{4,3,2,1,0:T(8,128)(2,1)S(1)}, bf16[8,2,32,16,128]{4,3,2,1,0:T(8,128)(2,1)}, u32[]{:S(2)}) copy-start(bf16[8,2,32,16,128]{4,3,2,1,0:T(8,128)(2,1)} %copy-done.1) | copy-start | bytes 6291460

commit v3 on v2

--- a/solution.py
+++ b/solution.py
@@ -6,6 +6,7 @@
 from jax.experimental import pallas as pl
 from jax.experimental.pallas import tpu as pltpu
 from jax.sharding import PartitionSpec as P
+
 
 COLS = 256
 ARC = 64
@@ -28,7 +29,6 @@
 ):
     beam = pl.program_id(0)
     pulses = ext_ref.shape[2]
-    cells = ext_ref.shape[3]
     num_sel = col_ref.shape[1]
     num_chan = bins_ref.shape[1]
     table = table_ref[...]
@@ -205,32 +205,25 @@
         def _(t=t):
             left_copy(t).start()
 
-    for s in range(n - 1):
-        t = n - 1 - s
-
-        @pl.when(jnp.logical_and(z > 0, z < t))
-        def _(t=t):
-            right_copy(t).wait_recv()
-            acc[t] = acc[t] + right[t]
-            right_copy(t).start()
-
-        @pl.when(jnp.logical_and(z < n - 1, z > s))
-        def _(t=s):
-            left_copy(t).wait_recv()
-            acc[t] = acc[t] + left[t]
-            left_copy(t).start()
-
-    for t in range(n):
-
-        @pl.when(z == t)
-        def _(t=t):
-            total = acc[t]
-            if t > 0:
-                right_copy(t).wait_recv()
-                total = total + right[t]
-            if t < n - 1:
-                left_copy(t).wait_recv()
-                total = total + left[t]
+    for place in range(n):
+        events = [(place + n - 1 - t, 0, t) for t in range(place + 1, n) if place > 0]
+        events += [(n - 1 - place + t, 1, t) for t in range(place) if place < n - 1]
+
+        @pl.when(z == place)
+        def _(place=place, events=sorted(events)):
+            for _, side, t in events:
+                copy = left_copy(t) if side else right_copy(t)
+                source = left if side else right
+                copy.wait_recv()
+                acc[t] = acc[t] + source[t]
+                copy.start()
+            total = acc[place]
+            if place > 0:
+                right_copy(place).wait_recv()
+                total = total + right[place]
+            if place < n - 1:
+                left_copy(place).wait_recv()
+                total = total + left[place]
             out_ref[...] = total
 
     for t in range(n):
@@ -254,8 +247,8 @@
     *refs,
 ):
     v_refs = refs[:halves]
-    (out_ref, v_all, gat, expand, power, edge, halo, sums, az_lo, az_hi) = refs[halves : halves + 10]
-    (vsem, gsend, grecv, esend, erecv, asend, arecv) = refs[halves + 10 :]
+    (out_ref, v_all, gat, power, edge, halo, sums, az_lo, az_hi) = refs[halves : halves + 9]
+    (vsem, gsend, grecv, esend, erecv, asend, arecv) = refs[halves + 9 :]
     me = lax.axis_index("rng")
     az = lax.axis_index("az")
     n = lax.axis_size("rng")
@@ -293,13 +286,6 @@
         copy.start()
         copies.append(copy)
     gat[me] = pay_ref[...]
-    depth = expand.shape[1]
-    wide = expand.shape[2]
-    src = lax.broadcasted_iota(jnp.int32, (depth, wide), 0)
-    dst = lax.broadcasted_iota(jnp.int32, (depth, wide), 1)
-    want = (dst // taps) * num_sel + dst % num_sel
-    expand[0] = (src == want).astype(jnp.float32).astype(jnp.bfloat16)
-    expand[1] = (src == want + dof).astype(jnp.float32).astype(jnp.bfloat16)
     for load in loads:
         load.wait()
     for copy in copies:
@@ -312,6 +298,8 @@
     for b in range(beams):
         sums[b, :1, :] = count[b : b + 1]
     freq = lax.broadcasted_iota(jnp.int32, (num_chan, taps), 1) // num_sel
+    lanes = gat.shape[2]
+    lane = lax.broadcasted_iota(jnp.int32, (num_chan, lanes), 1)
 
     def one(b, carry):
         if per >= num_chan:
@@ -323,15 +311,24 @@
             w = jnp.concatenate([gat[b * split + t, :per, :] for t in range(split)], 0)
         w = w * sums[b, :1, :]
         quiet = w[:, 2 * dof : 2 * dof + 1]
-        wb = w.astype(jnp.bfloat16)
         centre = bins_ref[b]
         planes = []
+        hits = []
+        for q in range(BINS):
+            f = lax.rem(centre + (q - BINS // 2 + pulses), pulses)
+            hits.append(freq == f)
         for part in range(2):
-            spread = jnp.dot(wb, expand[part], preferred_element_type=jnp.float32)
             plane = jnp.zeros((num_chan, taps), jnp.float32)
             for q in range(BINS):
-                f = lax.rem(centre + (q - BINS // 2 + pulses), pulses)
-                plane = jnp.where(freq == f, spread[:, q * taps : (q + 1) * taps], plane)
+                start = part * dof + q * num_sel
+                piece = pltpu.roll(w, (lanes - start) % lanes, 1) if start else w
+                piece = jnp.where(lane < num_sel, piece, 0.0)
+                span = num_sel
+                while span < lanes:
+                    piece = piece + pltpu.roll(piece, span, 1)
+                    span *= 2
+                tiled = jnp.concatenate([piece] * (taps // lanes), 1)
+                plane = jnp.where(hits[q], tiled, plane)
             planes.append(plane)
         top = jnp.concatenate([planes[0], planes[1]], 1)
         low = jnp.concatenate([-planes[1], planes[0]], 1)
@@ -481,6 +478,7 @@
     half = beam_count // 2
     if (half - 1) * step + step - 1 + ARC - 1 < width + columns and half * step >= width:
         v_lo, gram_lo = snap_gram(jnp.concatenate([low, echoes], 1), 0, half, 0)
+        high, v_lo, gram_lo = lax.optimization_barrier((high, v_lo, gram_lo))
         v_hi, gram_hi = snap_gram(jnp.concatenate([echoes, high], 1), half, beam_count, width)
         v_parts = (v_lo, v_hi)
         gram = jnp.concatenate([gram_lo, gram_hi], 0)
@@ -542,7 +540,6 @@
     )
     halves = len(v_parts)
     any_spec = pl.BlockSpec(memory_space=pl.ANY)
-    taps = num_pulses * num_sel
     block = (chan_count, cells)
     out = pl.pallas_call(
         functools.partial(apply_kernel, halves, per, dof),
@@ -552,7 +549,6 @@
         scratch_shapes=[
             vm((beam_count, 2, num_pulses, num_sel, cells), jnp.bfloat16),
             vm((rng_size,) + payload.shape, jnp.float32),
-            vm((2, lanes, BINS * taps), jnp.bfloat16),
             vm((beam_count,) + block, jnp.float32),
             vm((2, 8, item_count), jnp.float32),
             vm((2, 8, item_count), jnp.float32),

time: 119 us -> 112 us (0.941)
  waiting for transfers between devices: 22.1 us -> 15.1 us
  Pallas kernels: 77.3 us -> 75.6 us
    pallas_call x1, Pallas kernels: 36.1 us -> 28.4 us  [body(): pl.pallas_call(functools.partial(scatter_kernel, line), in_specs=[pl.Bloc...]
    ppermute x1, waiting for transfers between devices: 10.6 us -> 3.56 us  [body(): high = lax.ppermute(echoes[:, :width], 'az', backward)]
    pallas_call x1, Pallas kernels: 19.8 us -> 25.8 us  [body(): pl.pallas_call(functools.partial(apply_kernel, halves, per, dof), in_spec...]
    unnamed x20 -> x22, local copies, waits for them, and re-layouts: 3.83 us -> 3.83 us
  transfers between devices with their start and end apart: 2 -> 2, of which waited for: 2 -> 2; matrix products, arithmetic and copies ran while one was open for 1% -> 1% of each run, Pallas kernels for 0% -> 6%
where the time goes in v3:
time: 112 us
  Pallas kernels  75.6 us (67%)
  waiting for transfers between devices  15.1 us (13%)
  local copies, waits for them, and re-layouts  12.2 us (11%)
  other arithmetic  5.12 us (5%)
  starting transfers between devices  3.93 us (4%)
    pallas_call x1, Pallas kernels, body(): pl.pallas_call(functools.partial(scatter_kernel, line), in_specs=[pl.Bloc...  28.4 us
    pallas_call x1, Pallas kernels, body(): pl.pallas_call(functools.partial(apply_kernel, halves, per, dof), in_spec...  25.8 us
    pallas_call x2, Pallas kernels, snap_gram(): pl.pallas_call(snap_gram_kernel, grid=(share,), in_specs=[smem, smem, sme...  13.9 us
    ppermute x1, waiting for transfers between devices, body(): low = lax.ppermute(echoes[:, columns - width:], 'az', forward)  11.5 us
    pallas_call x1, Pallas kernels, body(): pl.pallas_call(solve_kernel, out_shape=jax.ShapeDtypeStruct((2 * dof + 8,...  7.55 us
    reshape x4, local copies, waits for them, and re-layouts, body(): part.reshape(lead, dof, width, dof).transpose(1, 3, 0, 2)  5.46 us
    unnamed x22, local copies, waits for them, and re-layouts  3.83 us
    ppermute x1, waiting for transfers between devices, body(): high = lax.ppermute(echoes[:, :width], 'az', backward)  3.56 us
  transfers between devices with their start and end apart: 2, of which 2 were waited for; matrix products, arithmetic and copies ran while one was open for 1% of the time, Pallas kernels for 6%

profile of v3, /device:TPU:0, one launch (start us, length us, event | category | flops | bytes accessed | tf_op | source)
XLA Modules:
  0.0 112.1 jit_solution(10232107386115584637)
XLA Ops:
  0.0 2.2 %fusion.10 = (bf16[2,32,32,128]{3,2,1,0:T(8,128)(2,1)S(1)}, bf16[2,32,32,128]{3,2,1,0:T(8,128)(2,1)}) fusion(bf16[2,64,32,128]{3,2,1,0:T(8,128)(2,1)} %param.6), kind=kLoop, calls=%fused_computation.37 | loop fusion | bytes 2097152 | tf_op jit(solution)/shard_map/slice | solution.py:475
  2.2 3.0 %collective-permute-start.1 = (bf16[2,32,32,128]{3,2,1,0:T(8,128)(2,1)S(1)}, bf16[2,32,32,128]{3,2,1,0:T(8,128)(2,1)S(1)}, u32[]{:S(2)}, u32[]{:S(2)}) collective-permute-start(bf16[2,32,32,128]{3,2,1,0:T(8,128)(2,1)S(1)} %get-tuple-element.21), channel_id=1, source_target_pairs={{0,8},{8,16},{16,24},{24,0},{1,9},{9,17},{17,25},{25,1},{2,10},{10... | collective-permute-start | bytes 1572872 | tf_op jit(solution)/shard_map/ppermute | solution.py:475
  5.2 1.0 collective-permute-start
  6.2 0.1 sine_convert_fusion
  6.3 0.1 fusion.8
  7.0 0.2 copy.21.bins_ref
  7.4 11.5 %collective-permute-done.1 = bf16[2,32,32,128]{3,2,1,0:T(8,128)(2,1)S(1)} collective-permute-done((bf16[2,32,32,128]{3,2,1,0:T(8,128)(2,1)S(1)}, bf16[2,32,32,128]{3,2,1,0:T(8,128)(2,1)S(1)}, u32[]{:S(2)}, u32[]{:S(2)}) %collective-permute-start.1) | collective-permute-done | bytes 524320 | tf_op jit(solution)/shard_map/ppermute | solution.py:475
  18.9 0.1 pad_maximum_fusion.1.ext_ref
  19.2 7.0 %snap_gram.2 = (bf16[8,2,32,16,128]{4,3,2,1,0:T(8,128)(2,1)S(1)}, f32[8,48,768]{2,1,0:T(8,128)S(1)}) custom-call(s32[8,16]{1,0:T(8,128)S(1)} %get-tuple-element.29.col_ref, s32[8,16]{1,0:T(8,128)S(1)} %get-tuple-element.27.bins_ref, f32[8,16]{1,0:T(8,128)S(1)} %get-tuple-element.40.cos_ref, f32[8,16]{1,0:T(8,128)S(1)} %get-tuple-element.23.sin_ref, ...), custom_call_target="tpu_custom_call" | custom-call | flops 4800000000 | bytes 12000000 | tf_op jit(solution)/shard_map/snap_gram/pallas_call | solution.py:437
  26.1 3.6 %collective-permute-done = bf16[2,32,32,128]{3,2,1,0:T(8,128)(2,1)} collective-permute-done((bf16[2,32,32,128]{3,2,1,0:T(8,128)(2,1)}, bf16[2,32,32,128]{3,2,1,0:T(8,128)(2,1)}, u32[]{:S(2)}, u32[]{:S(2)}) %collective-permute-start) | collective-permute-done | bytes 524320 | tf_op jit(solution)/shard_map/ppermute | solution.py:476
  29.7 1.2 %pad_maximum_fusion.2.ext_ref = bf16[2,96,32,128]{3,2,1,0:T(8,128)(2,1)S(1)} fusion(bf16[2,32,32,128]{3,2,1,0:T(8,128)(2,1)} %collective-permute-done, bf16[2,64,32,128]{3,2,1,0:T(8,128)(2,1)S(1)} %copy-done.4), kind=kLoop, calls=%fused_computation.2 | loop fusion | flops 786432 | bytes 3145728 | tf_op jit(solution)/shard_map/concatenate | solution.py:482
  30.9 6.9 %snap_gram.3 = (bf16[8,2,32,16,128]{4,3,2,1,0:T(8,128)(2,1)S(1)}, f32[8,48,768]{2,1,0:T(8,128)S(1)}) custom-call(s32[8,16]{1,0:T(8,128)S(1)} %get-tuple-element.30.col_ref, s32[8,16]{1,0:T(8,128)S(1)} %get-tuple-element.28.bins_ref, f32[8,16]{1,0:T(8,128)S(1)} %get-tuple-element.39.cos_ref, f32[8,16]{1,0:T(8,128)S(1)} %get-tuple-element.24.sin_ref, ...), custom_call_target="tpu_custom_call" | custom-call | flops 4800000000 | bytes 12000000 | tf_op jit(solution)/shard_map/snap_gram/pallas_call | solution.py:437
  37.9 1.3 %copy-done.1 = bf16[8,2,32,16,128]{4,3,2,1,0:T(8,128)(2,1)} copy-done((bf16[8,2,32,16,128]{4,3,2,1,0:T(8,128)(2,1)}, bf16[8,2,32,16,128]{4,3,2,1,0:T(8,128)(2,1)S(1)}, u32[]{:S(2)}) %copy-start.1) | copy-done | bytes 2097176
  39.2 0.2 pad_maximum_fusion
  39.4 28.4 %scatter.1 = f32[2,48,768]{2,1,0:T(8,128)S(1)} custom-call(f32[8,2,48,768]{3,2,1,0:T(8,128)S(1)} %bitcast.19), custom_call_target="tpu_custom_call" | custom-call | tf_op jit(solution)/shard_map/scatter/pallas_call | solution.py:501
  67.7 1.3 %reshape.65 = f32[2,48,16,48]{3,2,1,0:T(8,128)} reshape(f32[2,48,768]{2,1,0:T(8,128)S(1)} %scatter.1) | data formatting | bytes 589824 | tf_op jit(solution)/shard_map/reshape | solution.py:513
  69.0 1.2 %copy.16 = f32[2,48,16,48]{3,2,0,1:T(8,128)S(1)} copy(f32[2,48,16,48]{3,2,1,0:T(8,128)} %reshape.65) | data formatting | bytes 589824 | tf_op jit(solution)/shard_map/reshape | solution.py:513
  70.3 1.5 %copy.17 = f32[48,48,32]{2,0,1:T(8,128)} copy(f32[48,48,32]{1,2,0:T(8,128)S(1)} %bitcast.20) | data formatting | bytes 589824 | tf_op jit(solution)/shard_map/reshape | solution.py:513
  71.8 1.4 %copy.18 = f32[48,48,32]{2,1,0:T(8,128)} copy(f32[48,48,32]{1,2,0:T(8,128)S(1)} %bitcast.21) | data formatting | bytes 589824 | tf_op jit(solution)/shard_map/reshape | solution.py:513
  73.2 3.1 %fusion.1 = (f32[48,48,32]{2,1,0:T(8,128)S(1)}, f32[48,48,32]{2,1,0:T(8,128)S(1)}) fusion(f32[48,48,32]{2,1,0:T(8,128)} %copy.18, f32[48,48,32]{2,0,1:T(8,128)} %copy.17, pred[48,48]{1,0:T(8,128)(4,1)S(1)} %get-tuple-element.43, pred[48,48]{1,0:T(8,128)(4,1)S(1)} %get-tuple-element.44, pred[48,48]{1,0:T(8,128)(4,1)S(1)} %iota_compare_fusion.3), kind=kLoop, calls=%fused_computation.6 | loop fusion | flops 294912 | bytes 1186560 | tf_op jit(solution)/shard_map/jit(_where)/select_n | solution.py:518
  76.4 7.5 %solve.1 = f32[104,32]{1,0:T(8,128)S(1)} custom-call(f32[48,48,32]{2,1,0:T(8,128)S(1)} %get-tuple-element.20.hr_in, f32[48,48,32]{2,1,0:T(8,128)S(1)} %get-tuple-element.19.hi_in), custom_call_target="tpu_custom_call" | custom-call | tf_op jit(solution)/shard_map/solve/pallas_call | solution.py:519
  84.0 1.6 %copy-done.2 = bf16[8,2,32,16,128]{4,3,2,1,0:T(8,128)(2,1)S(1)} copy-done((bf16[8,2,32,16,128]{4,3,2,1,0:T(8,128)(2,1)S(1)}, bf16[8,2,32,16,128]{4,3,2,1,0:T(8,128)(2,1)}, u32[]{:S(2)}) %copy-start.2) | copy-done | bytes 2097176
  85.7 25.8 %apply.1 = f32[16,16,128]{2,1,0:T(8,128)S(1)} custom-call(f32[48,128]{1,0:T(8,128)S(1)} %select_maximum_fusion.pay_ref, s32[16,16,1]{2,1,0:T(8,128)S(1)} %copy.21.bins_ref, bf16[8,2,32,16,128]{4,3,2,1,0:T(8,128)(2,1)S(1)} %get-tuple-element.17.refs_0_, bf16[8,2,32,16,128]{4,3,2,1,0:T(8,128)(2,1)S(1)} %copy-done.2), custom_call_target="tpu_custom_call" | custom-call | tf_op jit(solution)/shard_map/apply/pallas_call | solution.py:544
  111.5 0.7 copy.26
  (37 shorter events, 1.2 us)
Async XLA Ops:
  0.0 6.4 %copy-start = (f32[64,16]{0,1:T(8,128)S(1)}, f32[64,16]{0,1:T(8,128)}, u32[]{:S(2)}) copy-start(f32[64,16]{0,1:T(8,128)} %param.10) | copy-start | bytes 12292
  0.0 18.9 %copy-start.3 = (bf16[2,64,32,128]{3,2,1,0:T(8,128)(2,1)S(1)}, bf16[2,64,32,128]{3,2,1,0:T(8,128)(2,1)}, u32[]{:S(2)}) copy-start(bf16[2,64,32,128]{3,2,1,0:T(8,128)(2,1)} %param.6) | copy-start | bytes 3145732
  0.0 6.5 %copy-start.6 = (s32[64,16]{0,1:T(8,128)S(1)}, s32[64,16]{0,1:T(8,128)}, u32[]{:S(2)}) copy-start(s32[64,16]{0,1:T(8,128)} %param.8) | copy-start | bytes 12292
  0.0 6.5 %copy-start.5 = (s32[64,16]{0,1:T(8,128)S(1)}, s32[64,16]{0,1:T(8,128)}, u32[]{:S(2)}) copy-start(s32[64,16]{0,1:T(8,128)} %param.9) | copy-start | bytes 12292
  0.0 6.7 %copy-start.7 = (s32[64]{0:T(128)S(1)}, s32[64]{0:T(128)}, u32[]{:S(2)}) copy-start(s32[64]{0:T(128)} %param.7) | copy-start | bytes 772
  0.0 6.9 %copy-start.8 = (s32[16,1]{0,1:T(1,128)S(1)}, s32[16,1]{0,1:T(1,128)}, u32[]{:S(2)}) copy-start(s32[16,1]{0,1:T(1,128)} %param.11) | copy-start | bytes 196
  2.2 16.7 %collective-permute-start.1 = (bf16[2,32,32,128]{3,2,1,0:T(8,128)(2,1)S(1)}, bf16[2,32,32,128]{3,2,1,0:T(8,128)(2,1)S(1)}, u32[]{:S(2)}, u32[]{:S(2)}) collective-permute-start(bf16[2,32,32,128]{3,2,1,0:T(8,128)(2,1)S(1)} %get-tuple-element.21), channel_id=1, source_target_pairs={{0,8},{8,16},{16,24},{24,0},{1,9},{9,17},{17,25},{25,1},{2,10},{10... | collective-permute-start | bytes 1572872 | tf_op jit(solution)/shard_map/ppermute | solution.py:475
  5.2 24.5 %collective-permute-start = (bf16[2,32,32,128]{3,2,1,0:T(8,128)(2,1)}, bf16[2,32,32,128]{3,2,1,0:T(8,128)(2,1)}, u32[]{:S(2)}, u32[]{:S(2)}) collective-permute-start(bf16[2,32,32,128]{3,2,1,0:T(8,128)(2,1)} %get-tuple-element.22), channel_id=1, source_target_pairs={{8,0},{16,8},{24,16},{0,24},{9,1},{17,9},{25,17},{1,25},{10,2},{18... | collective-permute-start | bytes 1572872 | tf_op jit(solution)/shard_map/ppermute | solution.py:476
  19.1 10.5 %copy-start.4 = (bf16[2,64,32,128]{3,2,1,0:T(8,128)(2,1)S(1)}, bf16[2,64,32,128]{3,2,1,0:T(8,128)(2,1)}, u32[]{:S(2)}) copy-start(bf16[2,64,32,128]{3,2,1,0:T(8,128)(2,1)} %param.6) | copy-start | bytes 3145732
  37.9 1.3 %copy-start.1 = (bf16[8,2,32,16,128]{4,3,2,1,0:T(8,128)(2,1)}, bf16[8,2,32,16,128]{4,3,2,1,0:T(8,128)(2,1)S(1)}, u32[]{:S(2)}) copy-start(bf16[8,2,32,16,128]{4,3,2,1,0:T(8,128)(2,1)S(1)} %get-tuple-element.18.refs_1_) | copy-start | bytes 6291460
  84.0 1.6 %copy-start.2 = (bf16[8,2,32,16,128]{4,3,2,1,0:T(8,128)(2,1)S(1)}, bf16[8,2,32,16,128]{4,3,2,1,0:T(8,128)(2,1)}, u32[]{:S(2)}) copy-start(bf16[8,2,32,16,128]{4,3,2,1,0:T(8,128)(2,1)} %copy-done.1) | copy-start | bytes 6291460

commit v4 on v3

--- a/solution.py
+++ b/solution.py
@@ -70,46 +70,70 @@
     gram_ref[0] = jnp.concatenate(packed, 1)
 
 
-def solve_kernel(hr_in, hi_in, out_ref, hr, hi, xr, xi):
-    dof = hr_in.shape[0]
-    lanes = hr_in.shape[2]
+def solve_kernel(part_ref, out_ref, stack, turned, h, x1, x2):
+    lead, dof, wide = part_ref.shape
+    width = wide // dof
+    lanes = lead * width
     nb = dof // 8
-    hr[:, :dof, :] = hr_in[...]
-    hi[:, :dof, :] = hi_in[...]
-    hr[:, dof:, :] = jnp.ones((dof, 8, lanes), jnp.float32)
-    hi[:, dof:, :] = jnp.zeros((dof, 8, lanes), jnp.float32)
-    xr[...] = jnp.zeros_like(xr)
-    xi[...] = jnp.zeros_like(xi)
+    group = min(8, lanes)
+    for g in range(0, lanes, group):
+        pieces = []
+        for item in range(g, g + group):
+            k = item % width
+            pieces.append(part_ref[item // width, :, k * dof : (k + 1) * dof])
+        stack[:, g : g + group, :] = jnp.swapaxes(jnp.stack(pieces, 0), 0, 1)
+    for i in range(dof):
+        turned[i] = stack[i].T
     trace = jnp.zeros((1, lanes), jnp.float32)
     for i in range(dof):
-        trace = trace + hr[i, i : i + 1, :]
+        trace = trace + turned[i, i : i + 1, :]
     load = (LOADING / dof) * trace
-    for i in range(dof):
-        hr[i, i : i + 1, :] = hr[i, i : i + 1, :] + load
-    sub = lax.broadcasted_iota(jnp.int32, (8, lanes), 0)
+    cube = (8, 8, lanes)
+    row = lax.broadcasted_iota(jnp.int32, cube, 0)
+    col = lax.broadcasted_iota(jnp.int32, cube, 1)
+    for ib in range(nb):
+        rows = slice(8 * ib, 8 * ib + 8)
+        for jb in range(ib, nb):
+            cols = slice(8 * jb, 8 * jb + 8)
+            imag = turned[rows, cols, :]
+            real = jnp.swapaxes(turned[cols, rows, :], 0, 1)
+            if ib == jb:
+                straight, flip = imag, real
+                real = jnp.where(row >= col, straight, flip)
+                real = jnp.where(row == col, real + load[None], real)
+                imag = jnp.where(row < col, straight, jnp.where(row > col, -flip, 0.0))
+            h[rows, cols, :] = jnp.concatenate([real, imag], 2)
+    h[:, dof:, :] = jnp.concatenate(
+        [jnp.ones((dof, 8, lanes), jnp.float32), jnp.zeros((dof, 8, lanes), jnp.float32)], 2
+    )
+    x1[...] = jnp.zeros_like(x1)
+    x2[...] = jnp.zeros_like(x2)
+    sub = lax.broadcasted_iota(jnp.int32, (8, 2 * lanes), 0)
 
     for kb in range(nb):
 
         def step(k, carry, kb=kb):
-            pivot = 1.0 / hr[k, pl.ds(k, 1), :]
-            rr = [hr[k, 8 * b : 8 * b + 8, :] for b in range(kb, nb + 1)]
-            ri = [hi[k, 8 * b : 8 * b + 8, :] for b in range(kb, nb + 1)]
+            pivot = 1.0 / h[k, pl.ds(k, 1), :][:, :lanes]
+            pivot = jnp.concatenate([pivot, pivot], 1)
+            straight = [h[k, 8 * b : 8 * b + 8, :] for b in range(kb, nb + 1)]
+            real = [p[:, :lanes] for p in straight]
+            imag = [p[:, lanes:] for p in straight]
+            turn = [jnp.concatenate([-i, r], 1) for r, i in zip(real, imag)]
             for ib in range(kb, nb):
-                fr = rr[ib - kb] * pivot
-                fi = -ri[ib - kb] * pivot
+                r, i = real[ib - kb], imag[ib - kb]
+                fr = jnp.concatenate([r, r], 1) * pivot
+                fi = jnp.concatenate([i, i], 1) * -pivot
                 if ib == kb:
                     live = sub + 8 * kb > k
                     fr = jnp.where(live, fr, 0.0)
                     fi = jnp.where(live, fi, 0.0)
                 for s in range(8):
-                    i = 8 * ib + s
-                    cr = jnp.broadcast_to(fr[s : s + 1], (8, lanes))
-                    ci = jnp.broadcast_to(fi[s : s + 1], (8, lanes))
+                    t = 8 * ib + s
+                    cr = jnp.broadcast_to(fr[s : s + 1], (8, 2 * lanes))
+                    ci = jnp.broadcast_to(fi[s : s + 1], (8, 2 * lanes))
                     for b in range(ib, nb + 1):
-                        pr, pi = rr[b - kb], ri[b - kb]
                         sl = slice(8 * b, 8 * b + 8)
-                        hr[i, sl, :] = hr[i, sl, :] - (cr * pr - ci * pi)
-                        hi[i, sl, :] = hi[i, sl, :] - (cr * pi + ci * pr)
+                        h[t, sl, :] = h[t, sl, :] - (cr * straight[b - kb] + ci * turn[b - kb])
             return carry
 
         lax.fori_loop(8 * kb, 8 * kb + 8, step, 0)
@@ -118,25 +142,28 @@
 
         def back(t, carry, ib=ib):
             i = 8 * ib + 7 - t
-            sr = jnp.zeros((8, lanes), jnp.float32)
-            si = jnp.zeros((8, lanes), jnp.float32)
+            u = jnp.zeros((8, 2 * lanes), jnp.float32)
+            v = jnp.zeros((8, 2 * lanes), jnp.float32)
             for b in range(ib, nb):
                 sl = slice(8 * b, 8 * b + 8)
-                ar, ai = hr[i, sl, :], hi[i, sl, :]
-                br, bi = xr[sl, :], xi[sl, :]
-                sr = sr + (ar * br - ai * bi)
-                si = si + (ar * bi + ai * br)
-            pivot = 1.0 / hr[i, pl.ds(i, 1), :]
-            top_r = hr[i, dof : dof + 1, :]
-            top_i = hi[i, dof : dof + 1, :]
-            xr[pl.ds(i, 1), :] = (top_r - jnp.sum(sr, 0, keepdims=True)) * pivot
-            xi[pl.ds(i, 1), :] = (top_i - jnp.sum(si, 0, keepdims=True)) * pivot
+                line = h[i, sl, :]
+                u = u + line * x1[sl, :]
+                v = v + line * x2[sl, :]
+            u = jnp.sum(u, 0, keepdims=True)
+            v = jnp.sum(v, 0, keepdims=True)
+            pivot = 1.0 / h[i, pl.ds(i, 1), :][:, :lanes]
+            top = h[i, dof : dof + 1, :]
+            re = (top[:, :lanes] - (u[:, :lanes] + u[:, lanes:])) * pivot
+            im = (top[:, lanes:] - (v[:, :lanes] + v[:, lanes:])) * pivot
+            x1[pl.ds(i, 1), :] = jnp.concatenate([re, -im], 1)
+            x2[pl.ds(i, 1), :] = jnp.concatenate([im, re], 1)
             return carry
 
         lax.fori_loop(0, 8, back, 0)
-    out_ref[:dof, :] = xr[...]
-    out_ref[dof : 2 * dof, :] = xi[...]
-    out_ref[2 * dof :, :] = jnp.broadcast_to(jnp.sum(xr[...], 0, keepdims=True), (8, lanes))
+    re = x1[:, :lanes]
+    out_ref[:dof, :] = re
+    out_ref[dof : 2 * dof, :] = x2[:, :lanes]
+    out_ref[2 * dof :, :] = jnp.broadcast_to(jnp.sum(re, 0, keepdims=True), (8, lanes))
 
 
 MESH = pl.DeviceIdType.MESH
@@ -509,25 +536,19 @@
         ),
         name="scatter",
     )(gram.reshape((rng_size,) + chunk))
-    lead = part.shape[0]
-    mats = part.reshape(lead, dof, width, dof).transpose(1, 3, 0, 2).reshape(dof, dof, per)
-    flip = jnp.swapaxes(mats, 0, 1)
-    ids = jnp.arange(dof, dtype=jnp.int32)
-    row, col = ids[:, None, None], ids[None, :, None]
-    h_re = jnp.where(row >= col, mats, flip)
-    h_im = jnp.where(row < col, mats, jnp.where(row > col, -flip, 0.0))
     solved = pl.pallas_call(
         solve_kernel,
         out_shape=jax.ShapeDtypeStruct((2 * dof + 8, per), jnp.float32),
         scratch_shapes=[
-            vm((dof, dof + 8, per), jnp.float32),
-            vm((dof, dof + 8, per), jnp.float32),
-            vm((dof, per), jnp.float32),
-            vm((dof, per), jnp.float32),
+            vm((dof, per, dof), jnp.float32),
+            vm((dof, dof, per), jnp.float32),
+            vm((dof, dof + 8, 2 * per), jnp.float32),
+            vm((dof, 2 * per), jnp.float32),
+            vm((dof, 2 * per), jnp.float32),
         ],
         compiler_params=pltpu.CompilerParams(vmem_limit_bytes=VMEM_LIMIT),
         name="solve",
-    )(h_re, h_im)
+    )(part)
     lanes = 128
     local_count = (BLK * jnp.sum(train_mask, axis=1)).astype(jnp.float32)
     pad_rows = -per % 8

time: 112 us -> 115 us (1.027)
  Pallas kernels: 75.6 us -> 87.3 us
  local copies, waits for them, and re-layouts: 12.2 us -> 6.76 us
  other arithmetic: 5.12 us -> 1.97 us
    pallas_call x1, Pallas kernels: 7.55 us -> 19.2 us  [body(): pl.pallas_call(solve_kernel, out_shape=jax.ShapeDtypeStruct((2 * dof + 8,...]
    reshape x4 -> x0, local copies, waits for them, and re-layouts: 5.46 us -> none  [body(): part.reshape(lead, dof, width, dof).transpose(1, 3, 0, 2)]
    select_n x1 -> x0, other arithmetic: 3.13 us -> none  [body(): h_im = jnp.where(row < col, mats, jnp.where(row > col, -flip, 0.0))]
    unnamed x22 -> x20, local copies, waits for them, and re-layouts: 3.83 us -> 3.84 us
where the time goes in v4:
time: 115 us
  Pallas kernels  87.3 us (76%)
  waiting for transfers between devices  15.1 us (13%)
  local copies, waits for them, and re-layouts  6.76 us (6%)
  starting transfers between devices  3.93 us (3%)
  other arithmetic  1.97 us (2%)
    pallas_call x1, Pallas kernels, body(): pl.pallas_call(functools.partial(scatter_kernel, line), in_specs=[pl.Bloc...  28.4 us
    pallas_call x1, Pallas kernels, body(): pl.pallas_call(functools.partial(apply_kernel, halves, per, dof), in_spec...  25.8 us
    pallas_call x1, Pallas kernels, body(): pl.pallas_call(solve_kernel, out_shape=jax.ShapeDtypeStruct((2 * dof + 8,...  19.2 us
    pallas_call x2, Pallas kernels, snap_gram(): pl.pallas_call(snap_gram_kernel, grid=(share,), in_specs=[smem, smem, sme...  13.9 us
    ppermute x1, waiting for transfers between devices, body(): low = lax.ppermute(echoes[:, columns - width:], 'az', forward)  11.5 us
    unnamed x20, local copies, waits for them, and re-layouts  3.84 us
    ppermute x1, waiting for transfers between devices, body(): high = lax.ppermute(echoes[:, :width], 'az', backward)  3.57 us
    ppermute x1, starting transfers between devices, body(): low = lax.ppermute(echoes[:, columns - width:], 'az', forward)  2.97 us
  transfers between devices with their start and end apart: 2, of which 2 were waited for; matrix products, arithmetic and copies ran while one was open for 1% of the time, Pallas kernels for 6%

profile of v4, /device:TPU:0, one launch (start us, length us, event | category | flops | bytes accessed | tf_op | source)
XLA Modules:
  0.0 115.2 jit_solution(11661040072583170201)
XLA Ops:
  0.0 2.2 %fusion.8 = (bf16[2,32,32,128]{3,2,1,0:T(8,128)(2,1)S(1)}, bf16[2,32,32,128]{3,2,1,0:T(8,128)(2,1)}) fusion(bf16[2,64,32,128]{3,2,1,0:T(8,128)(2,1)} %param.6), kind=kLoop, calls=%fused_computation.30 | loop fusion | bytes 2097152 | tf_op jit(solution)/shard_map/slice | solution.py:502
  2.2 3.0 %collective-permute-start.1 = (bf16[2,32,32,128]{3,2,1,0:T(8,128)(2,1)S(1)}, bf16[2,32,32,128]{3,2,1,0:T(8,128)(2,1)S(1)}, u32[]{:S(2)}, u32[]{:S(2)}) collective-permute-start(bf16[2,32,32,128]{3,2,1,0:T(8,128)(2,1)S(1)} %get-tuple-element.19), channel_id=1, source_target_pairs={{0,8},{8,16},{16,24},{24,0},{1,9},{9,17},{17,25},{25,1},{2,10},{10... | collective-permute-start | bytes 1572872 | tf_op jit(solution)/shard_map/ppermute | solution.py:502
  5.2 1.0 collective-permute-start
  6.2 0.1 sine_convert_fusion
  6.2 0.1 fusion.6
  6.3 0.1 constant_dynamic-slice_fusion
  6.6 0.1 and_select_fusion
  6.7 0.1 broadcast_add_fusion
  7.0 0.2 copy.15.bins_ref
  7.2 0.1 maximum_maximum_fusion.table_ref
  7.4 11.5 %collective-permute-done.1 = bf16[2,32,32,128]{3,2,1,0:T(8,128)(2,1)S(1)} collective-permute-done((bf16[2,32,32,128]{3,2,1,0:T(8,128)(2,1)S(1)}, bf16[2,32,32,128]{3,2,1,0:T(8,128)(2,1)S(1)}, u32[]{:S(2)}, u32[]{:S(2)}) %collective-permute-start.1) | collective-permute-done | bytes 524320 | tf_op jit(solution)/shard_map/ppermute | solution.py:502
  18.9 0.1 pad_maximum_fusion.1.ext_ref
  19.1 6.9 %snap_gram.2 = (bf16[8,2,32,16,128]{4,3,2,1,0:T(8,128)(2,1)S(1)}, f32[8,48,768]{2,1,0:T(8,128)S(1)}) custom-call(s32[8,16]{1,0:T(8,128)S(1)} %get-tuple-element.27.col_ref, s32[8,16]{1,0:T(8,128)S(1)} %get-tuple-element.25.bins_ref, f32[8,16]{1,0:T(8,128)S(1)} %get-tuple-element.38.cos_ref, f32[8,16]{1,0:T(8,128)S(1)} %get-tuple-element.21.sin_ref, ...), custom_call_target="tpu_custom_call" | custom-call | flops 4800000000 | bytes 12000000 | tf_op jit(solution)/shard_map/snap_gram/pallas_call | solution.py:464
  26.1 3.6 %collective-permute-done = bf16[2,32,32,128]{3,2,1,0:T(8,128)(2,1)} collective-permute-done((bf16[2,32,32,128]{3,2,1,0:T(8,128)(2,1)}, bf16[2,32,32,128]{3,2,1,0:T(8,128)(2,1)}, u32[]{:S(2)}, u32[]{:S(2)}) %collective-permute-start) | collective-permute-done | bytes 524320 | tf_op jit(solution)/shard_map/ppermute | solution.py:503
  29.7 1.2 %pad_maximum_fusion.2.ext_ref = bf16[2,96,32,128]{3,2,1,0:T(8,128)(2,1)S(1)} fusion(bf16[2,32,32,128]{3,2,1,0:T(8,128)(2,1)} %collective-permute-done, bf16[2,64,32,128]{3,2,1,0:T(8,128)(2,1)S(1)} %copy-done.3), kind=kLoop, calls=%fused_computation.2 | loop fusion | flops 786432 | bytes 3145728 | tf_op jit(solution)/shard_map/concatenate | solution.py:509
  30.9 6.9 %snap_gram.3 = (bf16[8,2,32,16,128]{4,3,2,1,0:T(8,128)(2,1)S(1)}, f32[8,48,768]{2,1,0:T(8,128)S(1)}) custom-call(s32[8,16]{1,0:T(8,128)S(1)} %get-tuple-element.28.col_ref, s32[8,16]{1,0:T(8,128)S(1)} %get-tuple-element.26.bins_ref, f32[8,16]{1,0:T(8,128)S(1)} %get-tuple-element.37.cos_ref, f32[8,16]{1,0:T(8,128)S(1)} %get-tuple-element.22.sin_ref, ...), custom_call_target="tpu_custom_call" | custom-call | flops 4800000000 | bytes 12000000 | tf_op jit(solution)/shard_map/snap_gram/pallas_call | solution.py:464
  37.9 1.3 %copy-done.1 = bf16[8,2,32,16,128]{4,3,2,1,0:T(8,128)(2,1)} copy-done((bf16[8,2,32,16,128]{4,3,2,1,0:T(8,128)(2,1)}, bf16[8,2,32,16,128]{4,3,2,1,0:T(8,128)(2,1)S(1)}, u32[]{:S(2)}) %copy-start.1) | copy-done | bytes 2097176
  39.2 0.2 pad_maximum_fusion
  39.4 28.4 %scatter.1.part_ref = f32[2,48,768]{2,1,0:T(8,128)S(1)} custom-call(f32[8,2,48,768]{3,2,1,0:T(8,128)S(1)} %bitcast.9), custom_call_target="tpu_custom_call" | custom-call | tf_op jit(solution)/shard_map/scatter/pallas_call | solution.py:528
  67.7 19.2 %solve.1 = f32[104,32]{1,0:T(8,128)S(1)} custom-call(f32[2,48,768]{2,1,0:T(8,128)S(1)} %scatter.1.part_ref), custom_call_target="tpu_custom_call" | custom-call | tf_op jit(solution)/shard_map/solve/pallas_call | solution.py:539
  87.0 0.1 select_maximum_fusion.pay_ref
  87.1 1.6 %copy-done.2 = bf16[8,2,32,16,128]{4,3,2,1,0:T(8,128)(2,1)S(1)} copy-done((bf16[8,2,32,16,128]{4,3,2,1,0:T(8,128)(2,1)S(1)}, bf16[8,2,32,16,128]{4,3,2,1,0:T(8,128)(2,1)}, u32[]{:S(2)}) %copy-start.2) | copy-done | bytes 2097176
  88.7 25.8 %apply.1 = f32[16,16,128]{2,1,0:T(8,128)S(1)} custom-call(f32[48,128]{1,0:T(8,128)S(1)} %select_maximum_fusion.pay_ref, s32[16,16,1]{2,1,0:T(8,128)S(1)} %copy.15.bins_ref, bf16[8,2,32,16,128]{4,3,2,1,0:T(8,128)(2,1)S(1)} %get-tuple-element.17.refs_0_, bf16[8,2,32,16,128]{4,3,2,1,0:T(8,128)(2,1)S(1)} %copy-done.2), custom_call_target="tpu_custom_call" | custom-call | tf_op jit(solution)/shard_map/apply/pallas_call | solution.py:565
  114.5 0.7 copy.20
  (28 shorter events, 0.7 us)
Async XLA Ops:
  0.0 6.3 %copy-start = (f32[64,16]{0,1:T(8,128)S(1)}, f32[64,16]{0,1:T(8,128)}, u32[]{:S(2)}) copy-start(f32[64,16]{0,1:T(8,128)} %param.10) | copy-start | bytes 12292
  0.0 18.9 %copy-start.3 = (bf16[2,64,32,128]{3,2,1,0:T(8,128)(2,1)S(1)}, bf16[2,64,32,128]{3,2,1,0:T(8,128)(2,1)}, u32[]{:S(2)}) copy-start(bf16[2,64,32,128]{3,2,1,0:T(8,128)(2,1)} %param.6) | copy-start | bytes 3145732
  0.0 6.5 %copy-start.5 = (s32[64,16]{0,1:T(8,128)S(1)}, s32[64,16]{0,1:T(8,128)}, u32[]{:S(2)}) copy-start(s32[64,16]{0,1:T(8,128)} %param.8) | copy-start | bytes 12292
  0.0 6.5 %copy-start.4 = (s32[64,16]{0,1:T(8,128)S(1)}, s32[64,16]{0,1:T(8,128)}, u32[]{:S(2)}) copy-start(s32[64,16]{0,1:T(8,128)} %param.9) | copy-start | bytes 12292
  0.0 6.6 %copy-start.6 = (s32[64]{0:T(128)S(1)}, s32[64]{0:T(128)}, u32[]{:S(2)}) copy-start(s32[64]{0:T(128)} %param.7) | copy-start | bytes 772
  0.0 6.9 %copy-start.7 = (s32[16,1]{0,1:T(1,128)S(1)}, s32[16,1]{0,1:T(1,128)}, u32[]{:S(2)}) copy-start(s32[16,1]{0,1:T(1,128)} %param.11) | copy-start | bytes 196
  2.2 16.7 %collective-permute-start.1 = (bf16[2,32,32,128]{3,2,1,0:T(8,128)(2,1)S(1)}, bf16[2,32,32,128]{3,2,1,0:T(8,128)(2,1)S(1)}, u32[]{:S(2)}, u32[]{:S(2)}) collective-permute-start(bf16[2,32,32,128]{3,2,1,0:T(8,128)(2,1)S(1)} %get-tuple-element.19), channel_id=1, source_target_pairs={{0,8},{8,16},{16,24},{24,0},{1,9},{9,17},{17,25},{25,1},{2,10},{10... | collective-permute-start | bytes 1572872 | tf_op jit(solution)/shard_map/ppermute | solution.py:502
  5.2 24.5 %collective-permute-start = (bf16[2,32,32,128]{3,2,1,0:T(8,128)(2,1)}, bf16[2,32,32,128]{3,2,1,0:T(8,128)(2,1)}, u32[]{:S(2)}, u32[]{:S(2)}) collective-permute-start(bf16[2,32,32,128]{3,2,1,0:T(8,128)(2,1)} %get-tuple-element.20), channel_id=1, source_target_pairs={{8,0},{16,8},{24,16},{0,24},{9,1},{17,9},{25,17},{1,25},{10,2},{18... | collective-permute-start | bytes 1572872 | tf_op jit(solution)/shard_map/ppermute | solution.py:503
  37.9 1.3 %copy-start.1 = (bf16[8,2,32,16,128]{4,3,2,1,0:T(8,128)(2,1)}, bf16[8,2,32,16,128]{4,3,2,1,0:T(8,128)(2,1)S(1)}, u32[]{:S(2)}) copy-start(bf16[8,2,32,16,128]{4,3,2,1,0:T(8,128)(2,1)S(1)} %get-tuple-element.18.refs_1_) | copy-start | bytes 6291460
  87.1 1.6 %copy-start.2 = (bf16[8,2,32,16,128]{4,3,2,1,0:T(8,128)(2,1)S(1)}, bf16[8,2,32,16,128]{4,3,2,1,0:T(8,128)(2,1)}, u32[]{:S(2)}) copy-start(bf16[8,2,32,16,128]{4,3,2,1,0:T(8,128)(2,1)} %copy-done.1) | copy-start | bytes 6291460

commit v5 on v3

--- a/solution.py
+++ b/solution.py
@@ -70,22 +70,44 @@
     gram_ref[0] = jnp.concatenate(packed, 1)
 
 
-def solve_kernel(hr_in, hi_in, out_ref, hr, hi, xr, xi):
-    dof = hr_in.shape[0]
-    lanes = hr_in.shape[2]
+def solve_kernel(part_ref, out_ref, stack, turned, hr, hi, xr, xi):
+    lead, dof, wide = part_ref.shape
+    width = wide // dof
+    lanes = lead * width
     nb = dof // 8
-    hr[:, :dof, :] = hr_in[...]
-    hi[:, :dof, :] = hi_in[...]
+    group = min(8, lanes)
+    for g in range(0, lanes, group):
+        pieces = []
+        for item in range(g, g + group):
+            k = item % width
+            pieces.append(part_ref[item // width, :, k * dof : (k + 1) * dof])
+        stack[:, g : g + group, :] = jnp.swapaxes(jnp.stack(pieces, 0), 0, 1)
+    for i in range(dof):
+        turned[i] = stack[i].T
+    trace = jnp.zeros((1, lanes), jnp.float32)
+    for i in range(dof):
+        trace = trace + turned[i, i : i + 1, :]
+    load = (LOADING / dof) * trace
+    cube = (8, 8, lanes)
+    row = lax.broadcasted_iota(jnp.int32, cube, 0)
+    col = lax.broadcasted_iota(jnp.int32, cube, 1)
+    for ib in range(nb):
+        rows = slice(8 * ib, 8 * ib + 8)
+        for jb in range(ib, nb):
+            cols = slice(8 * jb, 8 * jb + 8)
+            imag = turned[rows, cols, :]
+            real = jnp.swapaxes(turned[cols, rows, :], 0, 1)
+            if ib == jb:
+                straight, flip = imag, real
+                real = jnp.where(row >= col, straight, flip)
+                real = jnp.where(row == col, real + load[None], real)
+                imag = jnp.where(row < col, straight, jnp.where(row > col, -flip, 0.0))
+            hr[rows, cols, :] = real
+            hi[rows, cols, :] = imag
     hr[:, dof:, :] = jnp.ones((dof, 8, lanes), jnp.float32)
     hi[:, dof:, :] = jnp.zeros((dof, 8, lanes), jnp.float32)
     xr[...] = jnp.zeros_like(xr)
     xi[...] = jnp.zeros_like(xi)
-    trace = jnp.zeros((1, lanes), jnp.float32)
-    for i in range(dof):
-        trace = trace + hr[i, i : i + 1, :]
-    load = (LOADING / dof) * trace
-    for i in range(dof):
-        hr[i, i : i + 1, :] = hr[i, i : i + 1, :] + load
     sub = lax.broadcasted_iota(jnp.int32, (8, lanes), 0)
 
     for kb in range(nb):
@@ -509,17 +531,12 @@
         ),
         name="scatter",
     )(gram.reshape((rng_size,) + chunk))
-    lead = part.shape[0]
-    mats = part.reshape(lead, dof, width, dof).transpose(1, 3, 0, 2).reshape(dof, dof, per)
-    flip = jnp.swapaxes(mats, 0, 1)
-    ids = jnp.arange(dof, dtype=jnp.int32)
-    row, col = ids[:, None, None], ids[None, :, None]
-    h_re = jnp.where(row >= col, mats, flip)
-    h_im = jnp.where(row < col, mats, jnp.where(row > col, -flip, 0.0))
     solved = pl.pallas_call(
         solve_kernel,
         out_shape=jax.ShapeDtypeStruct((2 * dof + 8, per), jnp.float32),
         scratch_shapes=[
+            vm((dof, per, dof), jnp.float32),
+            vm((dof, dof, per), jnp.float32),
             vm((dof, dof + 8, per), jnp.float32),
             vm((dof, dof + 8, per), jnp.float32),
             vm((dof, per), jnp.float32),
@@ -527,7 +544,7 @@
         ],
         compiler_params=pltpu.CompilerParams(vmem_limit_bytes=VMEM_LIMIT),
         name="solve",
-    )(h_re, h_im)
+    )(part)
     lanes = 128
     local_count = (BLK * jnp.sum(train_mask, axis=1)).astype(jnp.float32)
     pad_rows = -per % 8

time: 112 us -> 104 us (0.929)
  local copies, waits for them, and re-layouts: 12.2 us -> 6.76 us
  other arithmetic: 5.12 us -> 1.97 us
    reshape x4 -> x0, local copies, waits for them, and re-layouts: 5.46 us -> none  [body(): part.reshape(lead, dof, width, dof).transpose(1, 3, 0, 2)]
    select_n x1 -> x0, other arithmetic: 3.13 us -> none  [body(): h_im = jnp.where(row < col, mats, jnp.where(row > col, -flip, 0.0))]
    unnamed x22 -> x20, local copies, waits for them, and re-layouts: 3.83 us -> 3.84 us
  transfers between devices with their start and end apart: 2 -> 2, of which waited for: 2 -> 2; matrix products, arithmetic and copies ran while one was open for 1% -> 1% of each run, Pallas kernels for 6% -> 7%
where the time goes in v5:
time: 104 us
  Pallas kernels  76.3 us (73%)
  waiting for transfers between devices  15.1 us (15%)
  local copies, waits for them, and re-layouts  6.76 us (6%)
  starting transfers between devices  3.93 us (4%)
  other arithmetic  1.97 us (2%)
    pallas_call x1, Pallas kernels, body(): pl.pallas_call(functools.partial(scatter_kernel, line), in_specs=[pl.Bloc...  28.4 us
    pallas_call x1, Pallas kernels, body(): pl.pallas_call(functools.partial(apply_kernel, halves, per, dof), in_spec...  25.8 us
    pallas_call x2, Pallas kernels, snap_gram(): pl.pallas_call(snap_gram_kernel, grid=(share,), in_specs=[smem, smem, sme...  13.9 us
    ppermute x1, waiting for transfers between devices, body(): low = lax.ppermute(echoes[:, columns - width:], 'az', forward)  11.5 us
    pallas_call x1, Pallas kernels, body(): pl.pallas_call(solve_kernel, out_shape=jax.ShapeDtypeStruct((2 * dof + 8,...  8.19 us
    unnamed x20, local copies, waits for them, and re-layouts  3.84 us
    ppermute x1, waiting for transfers between devices, body(): high = lax.ppermute(echoes[:, :width], 'az', backward)  3.57 us
    ppermute x1, starting transfers between devices, body(): low = lax.ppermute(echoes[:, columns - width:], 'az', forward)  2.97 us
  transfers between devices with their start and end apart: 2, of which 2 were waited for; matrix products, arithmetic and copies ran while one was open for 1% of the time, Pallas kernels for 7%

profile of v5, /device:TPU:0, one launch (start us, length us, event | category | flops | bytes accessed | tf_op | source)
XLA Modules:
  0.0 104.2 jit_solution(16365410942464635076)
XLA Ops:
  0.0 2.2 %fusion.8 = (bf16[2,32,32,128]{3,2,1,0:T(8,128)(2,1)S(1)}, bf16[2,32,32,128]{3,2,1,0:T(8,128)(2,1)}) fusion(bf16[2,64,32,128]{3,2,1,0:T(8,128)(2,1)} %param.6), kind=kLoop, calls=%fused_computation.30 | loop fusion | bytes 2097152 | tf_op jit(solution)/shard_map/slice | solution.py:497
  2.2 3.0 %collective-permute-start.1 = (bf16[2,32,32,128]{3,2,1,0:T(8,128)(2,1)S(1)}, bf16[2,32,32,128]{3,2,1,0:T(8,128)(2,1)S(1)}, u32[]{:S(2)}, u32[]{:S(2)}) collective-permute-start(bf16[2,32,32,128]{3,2,1,0:T(8,128)(2,1)S(1)} %get-tuple-element.19), channel_id=1, source_target_pairs={{0,8},{8,16},{16,24},{24,0},{1,9},{9,17},{17,25},{25,1},{2,10},{10... | collective-permute-start | bytes 1572872 | tf_op jit(solution)/shard_map/ppermute | solution.py:497
  5.2 1.0 collective-permute-start
  6.2 0.1 sine_convert_fusion
  6.2 0.1 fusion.6
  6.3 0.1 constant_dynamic-slice_fusion
  6.6 0.1 and_select_fusion
  6.7 0.1 broadcast_add_fusion
  7.0 0.2 copy.15.bins_ref
  7.2 0.1 maximum_maximum_fusion.table_ref
  7.4 11.5 %collective-permute-done.1 = bf16[2,32,32,128]{3,2,1,0:T(8,128)(2,1)S(1)} collective-permute-done((bf16[2,32,32,128]{3,2,1,0:T(8,128)(2,1)S(1)}, bf16[2,32,32,128]{3,2,1,0:T(8,128)(2,1)S(1)}, u32[]{:S(2)}, u32[]{:S(2)}) %collective-permute-start.1) | collective-permute-done | bytes 524320 | tf_op jit(solution)/shard_map/ppermute | solution.py:497
  18.9 0.1 pad_maximum_fusion.1.ext_ref
  19.1 6.9 %snap_gram.2 = (bf16[8,2,32,16,128]{4,3,2,1,0:T(8,128)(2,1)S(1)}, f32[8,48,768]{2,1,0:T(8,128)S(1)}) custom-call(s32[8,16]{1,0:T(8,128)S(1)} %get-tuple-element.27.col_ref, s32[8,16]{1,0:T(8,128)S(1)} %get-tuple-element.25.bins_ref, f32[8,16]{1,0:T(8,128)S(1)} %get-tuple-element.38.cos_ref, f32[8,16]{1,0:T(8,128)S(1)} %get-tuple-element.21.sin_ref, ...), custom_call_target="tpu_custom_call" | custom-call | flops 4800000000 | bytes 12000000 | tf_op jit(solution)/shard_map/snap_gram/pallas_call | solution.py:459
  26.1 3.6 %collective-permute-done = bf16[2,32,32,128]{3,2,1,0:T(8,128)(2,1)} collective-permute-done((bf16[2,32,32,128]{3,2,1,0:T(8,128)(2,1)}, bf16[2,32,32,128]{3,2,1,0:T(8,128)(2,1)}, u32[]{:S(2)}, u32[]{:S(2)}) %collective-permute-start) | collective-permute-done | bytes 524320 | tf_op jit(solution)/shard_map/ppermute | solution.py:498
  29.7 1.2 %pad_maximum_fusion.2.ext_ref = bf16[2,96,32,128]{3,2,1,0:T(8,128)(2,1)S(1)} fusion(bf16[2,32,32,128]{3,2,1,0:T(8,128)(2,1)} %collective-permute-done, bf16[2,64,32,128]{3,2,1,0:T(8,128)(2,1)S(1)} %copy-done.3), kind=kLoop, calls=%fused_computation.2 | loop fusion | flops 786432 | bytes 3145728 | tf_op jit(solution)/shard_map/concatenate | solution.py:504
  30.9 6.9 %snap_gram.3 = (bf16[8,2,32,16,128]{4,3,2,1,0:T(8,128)(2,1)S(1)}, f32[8,48,768]{2,1,0:T(8,128)S(1)}) custom-call(s32[8,16]{1,0:T(8,128)S(1)} %get-tuple-element.28.col_ref, s32[8,16]{1,0:T(8,128)S(1)} %get-tuple-element.26.bins_ref, f32[8,16]{1,0:T(8,128)S(1)} %get-tuple-element.37.cos_ref, f32[8,16]{1,0:T(8,128)S(1)} %get-tuple-element.22.sin_ref, ...), custom_call_target="tpu_custom_call" | custom-call | flops 4800000000 | bytes 12000000 | tf_op jit(solution)/shard_map/snap_gram/pallas_call | solution.py:459
  37.9 1.3 %copy-done.1 = bf16[8,2,32,16,128]{4,3,2,1,0:T(8,128)(2,1)} copy-done((bf16[8,2,32,16,128]{4,3,2,1,0:T(8,128)(2,1)}, bf16[8,2,32,16,128]{4,3,2,1,0:T(8,128)(2,1)S(1)}, u32[]{:S(2)}) %copy-start.1) | copy-done | bytes 2097176
  39.2 0.2 pad_maximum_fusion
  39.4 28.4 %scatter.1.part_ref = f32[2,48,768]{2,1,0:T(8,128)S(1)} custom-call(f32[8,2,48,768]{3,2,1,0:T(8,128)S(1)} %bitcast.9), custom_call_target="tpu_custom_call" | custom-call | tf_op jit(solution)/shard_map/scatter/pallas_call | solution.py:523
  67.7 8.2 %solve.1 = f32[104,32]{1,0:T(8,128)S(1)} custom-call(f32[2,48,768]{2,1,0:T(8,128)S(1)} %scatter.1.part_ref), custom_call_target="tpu_custom_call" | custom-call | tf_op jit(solution)/shard_map/solve/pallas_call | solution.py:534
  76.0 0.1 select_maximum_fusion.pay_ref
  76.1 1.6 %copy-done.2 = bf16[8,2,32,16,128]{4,3,2,1,0:T(8,128)(2,1)S(1)} copy-done((bf16[8,2,32,16,128]{4,3,2,1,0:T(8,128)(2,1)S(1)}, bf16[8,2,32,16,128]{4,3,2,1,0:T(8,128)(2,1)}, u32[]{:S(2)}) %copy-start.2) | copy-done | bytes 2097176
  77.7 25.8 %apply.1 = f32[16,16,128]{2,1,0:T(8,128)S(1)} custom-call(f32[48,128]{1,0:T(8,128)S(1)} %select_maximum_fusion.pay_ref, s32[16,16,1]{2,1,0:T(8,128)S(1)} %copy.15.bins_ref, bf16[8,2,32,16,128]{4,3,2,1,0:T(8,128)(2,1)S(1)} %get-tuple-element.17.refs_0_, bf16[8,2,32,16,128]{4,3,2,1,0:T(8,128)(2,1)S(1)} %copy-done.2), custom_call_target="tpu_custom_call" | custom-call | tf_op jit(solution)/shard_map/apply/pallas_call | solution.py:561
  103.5 0.7 copy.20
  (28 shorter events, 0.7 us)
Async XLA Ops:
  0.0 6.3 %copy-start = (f32[64,16]{0,1:T(8,128)S(1)}, f32[64,16]{0,1:T(8,128)}, u32[]{:S(2)}) copy-start(f32[64,16]{0,1:T(8,128)} %param.10) | copy-start | bytes 12292
  0.0 18.9 %copy-start.3 = (bf16[2,64,32,128]{3,2,1,0:T(8,128)(2,1)S(1)}, bf16[2,64,32,128]{3,2,1,0:T(8,128)(2,1)}, u32[]{:S(2)}) copy-start(bf16[2,64,32,128]{3,2,1,0:T(8,128)(2,1)} %param.6) | copy-start | bytes 3145732
  0.0 6.5 %copy-start.5 = (s32[64,16]{0,1:T(8,128)S(1)}, s32[64,16]{0,1:T(8,128)}, u32[]{:S(2)}) copy-start(s32[64,16]{0,1:T(8,128)} %param.8) | copy-start | bytes 12292
  0.0 6.5 %copy-start.4 = (s32[64,16]{0,1:T(8,128)S(1)}, s32[64,16]{0,1:T(8,128)}, u32[]{:S(2)}) copy-start(s32[64,16]{0,1:T(8,128)} %param.9) | copy-start | bytes 12292
  0.0 6.6 %copy-start.6 = (s32[64]{0:T(128)S(1)}, s32[64]{0:T(128)}, u32[]{:S(2)}) copy-start(s32[64]{0:T(128)} %param.7) | copy-start | bytes 772
  0.0 6.9 %copy-start.7 = (s32[16,1]{0,1:T(1,128)S(1)}, s32[16,1]{0,1:T(1,128)}, u32[]{:S(2)}) copy-start(s32[16,1]{0,1:T(1,128)} %param.11) | copy-start | bytes 196
  2.2 16.7 %collective-permute-start.1 = (bf16[2,32,32,128]{3,2,1,0:T(8,128)(2,1)S(1)}, bf16[2,32,32,128]{3,2,1,0:T(8,128)(2,1)S(1)}, u32[]{:S(2)}, u32[]{:S(2)}) collective-permute-start(bf16[2,32,32,128]{3,2,1,0:T(8,128)(2,1)S(1)} %get-tuple-element.19), channel_id=1, source_target_pairs={{0,8},{8,16},{16,24},{24,0},{1,9},{9,17},{17,25},{25,1},{2,10},{10... | collective-permute-start | bytes 1572872 | tf_op jit(solution)/shard_map/ppermute | solution.py:497
  5.2 24.5 %collective-permute-start = (bf16[2,32,32,128]{3,2,1,0:T(8,128)(2,1)}, bf16[2,32,32,128]{3,2,1,0:T(8,128)(2,1)}, u32[]{:S(2)}, u32[]{:S(2)}) collective-permute-start(bf16[2,32,32,128]{3,2,1,0:T(8,128)(2,1)} %get-tuple-element.20), channel_id=1, source_target_pairs={{8,0},{16,8},{24,16},{0,24},{9,1},{17,9},{25,17},{1,25},{10,2},{18... | collective-permute-start | bytes 1572872 | tf_op jit(solution)/shard_map/ppermute | solution.py:498
  37.9 1.3 %copy-start.1 = (bf16[8,2,32,16,128]{4,3,2,1,0:T(8,128)(2,1)}, bf16[8,2,32,16,128]{4,3,2,1,0:T(8,128)(2,1)S(1)}, u32[]{:S(2)}) copy-start(bf16[8,2,32,16,128]{4,3,2,1,0:T(8,128)(2,1)S(1)} %get-tuple-element.18.refs_1_) | copy-start | bytes 6291460
  76.1 1.6 %copy-start.2 = (bf16[8,2,32,16,128]{4,3,2,1,0:T(8,128)(2,1)S(1)}, bf16[8,2,32,16,128]{4,3,2,1,0:T(8,128)(2,1)}, u32[]{:S(2)}) copy-start(bf16[8,2,32,16,128]{4,3,2,1,0:T(8,128)(2,1)} %copy-done.1) | copy-start | bytes 6291460

commit v6 on v5

--- a/solution.py
+++ b/solution.py
@@ -164,7 +164,14 @@
 MESH = pl.DeviceIdType.MESH
 
 
-def scatter_kernel(n, g_ref, out_ref, pair, acc, right, left, psend, precv, rsend, rrecv, lsend, lrecv):
+def scatter_kernel(n, halves, *refs):
+    g_refs = refs[:halves]
+    out_ref, pair, acc, right, left, psend, precv, rsend, rrecv, lsend, lrecv = refs[halves:]
+    share = n // halves
+
+    def own(t, core):
+        return g_refs[t // share].at[2 * (t % share) + core]
+
     me = lax.axis_index("rng")
     z = me // 2
     c = me % 2
@@ -185,7 +192,7 @@
 
     def pair_copy(t):
         return pltpu.make_async_remote_copy(
-            src_ref=g_ref.at[2 * t + 1 - c],
+            src_ref=own(t, 1 - c),
             dst_ref=pair.at[t],
             send_sem=psend.at[t],
             recv_sem=precv.at[t],
@@ -217,7 +224,7 @@
         pair_copy(t).start()
     for t in order:
         pair_copy(t).wait_recv()
-        acc[t] = g_ref[2 * t + c] + pair[t]
+        acc[t] = own(t, c)[...] + pair[t]
 
         @pl.when(jnp.logical_and(z == 0, t > 0))
         def _(t=t):
@@ -503,26 +510,29 @@
         high, v_lo, gram_lo = lax.optimization_barrier((high, v_lo, gram_lo))
         v_hi, gram_hi = snap_gram(jnp.concatenate([echoes, high], 1), half, beam_count, width)
         v_parts = (v_lo, v_hi)
-        gram = jnp.concatenate([gram_lo, gram_hi], 0)
+        grams = (gram_lo, gram_hi)
+        if rng_size % 4 or item_count // rng_size < chan_count:
+            grams = (jnp.concatenate(grams, 0),)
     else:
-        v_one, gram = snap_gram(jnp.concatenate([low, echoes, high], 1), 0, beam_count, 0)
+        v_one, gram_one = snap_gram(jnp.concatenate([low, echoes, high], 1), 0, beam_count, 0)
         v_parts = (v_one,)
+        grams = (gram_one,)
 
     per = item_count // rng_size
     if per < chan_count:
         split = chan_count // per
-        gram = gram.reshape(beam_count, dof, split, per * dof)
-        gram = jnp.swapaxes(gram, 1, 2).reshape(beam_count * split, dof, per * dof)
+        gram = grams[0].reshape(beam_count, dof, split, per * dof)
+        grams = (jnp.swapaxes(gram, 1, 2).reshape(beam_count * split, dof, per * dof),)
         width = per
     else:
         width = chan_count
     vm = pltpu.VMEM
     dma = pltpu.SemaphoreType.DMA
     line = rng_size // 2
-    chunk = (gram.shape[0] // rng_size, dof, gram.shape[2])
+    chunk = (grams[0].shape[0] * len(grams) // rng_size, dof, grams[0].shape[2])
     part = pl.pallas_call(
-        functools.partial(scatter_kernel, line),
-        in_specs=[pl.BlockSpec(memory_space=vm)],
+        functools.partial(scatter_kernel, line, len(grams)),
+        in_specs=[pl.BlockSpec(memory_space=vm)] * len(grams),
         out_specs=pl.BlockSpec(memory_space=vm),
         out_shape=jax.ShapeDtypeStruct(chunk, jnp.float32),
         scratch_shapes=[vm((line,) + chunk, jnp.float32)] * 4 + [dma((line,))] * 6,
@@ -530,7 +540,7 @@
             collective_id=0, has_side_effects=True, vmem_limit_bytes=VMEM_LIMIT
         ),
         name="scatter",
-    )(gram.reshape((rng_size,) + chunk))
+    )(*[g.reshape((rng_size // len(grams),) + chunk) for g in grams])
     solved = pl.pallas_call(
         solve_kernel,
         out_shape=jax.ShapeDtypeStruct((2 * dof + 8, per), jnp.float32),

time: 104 us -> 104 us (level)
  no operation moved by 1% of the time
where the time goes in v6:
time: 104 us
  Pallas kernels  76.2 us (73%)
  waiting for transfers between devices  15.1 us (15%)
  local copies, waits for them, and re-layouts  6.76 us (6%)
  starting transfers between devices  3.93 us (4%)
  other arithmetic  1.82 us (2%)
    pallas_call x1, Pallas kernels, body(): pl.pallas_call(functools.partial(scatter_kernel, line, len(grams)), in_sp...  28.3 us
    pallas_call x1, Pallas kernels, body(): pl.pallas_call(functools.partial(apply_kernel, halves, per, dof), in_spec...  25.8 us
    pallas_call x2, Pallas kernels, snap_gram(): pl.pallas_call(snap_gram_kernel, grid=(share,), in_specs=[smem, smem, sme...  13.9 us
    ppermute x1, waiting for transfers between devices, body(): low = lax.ppermute(echoes[:, columns - width:], 'az', forward)  11.5 us
    pallas_call x1, Pallas kernels, body(): pl.pallas_call(solve_kernel, out_shape=jax.ShapeDtypeStruct((2 * dof + 8,...  8.19 us
    unnamed x20, local copies, waits for them, and re-layouts  3.84 us
    ppermute x1, waiting for transfers between devices, body(): high = lax.ppermute(echoes[:, :width], 'az', backward)  3.57 us
    ppermute x1, starting transfers between devices, body(): low = lax.ppermute(echoes[:, columns - width:], 'az', forward)  2.97 us
  transfers between devices with their start and end apart: 2, of which 2 were waited for; matrix products, arithmetic and copies ran while one was open for 1% of the time, Pallas kernels for 7%

profile of v6, /device:TPU:0, one launch (start us, length us, event | category | flops | bytes accessed | tf_op | source)
XLA Modules:
  0.0 103.9 jit_solution(5753666841299781103)
XLA Ops:
  0.0 2.2 %fusion.8 = (bf16[2,32,32,128]{3,2,1,0:T(8,128)(2,1)S(1)}, bf16[2,32,32,128]{3,2,1,0:T(8,128)(2,1)}) fusion(bf16[2,64,32,128]{3,2,1,0:T(8,128)(2,1)} %param.6), kind=kLoop, calls=%fused_computation.29 | loop fusion | bytes 2097152 | tf_op jit(solution)/shard_map/slice | solution.py:504
  2.2 3.0 %collective-permute-start.1 = (bf16[2,32,32,128]{3,2,1,0:T(8,128)(2,1)S(1)}, bf16[2,32,32,128]{3,2,1,0:T(8,128)(2,1)S(1)}, u32[]{:S(2)}, u32[]{:S(2)}) collective-permute-start(bf16[2,32,32,128]{3,2,1,0:T(8,128)(2,1)S(1)} %get-tuple-element.19), channel_id=1, source_target_pairs={{0,8},{8,16},{16,24},{24,0},{1,9},{9,17},{17,25},{25,1},{2,10},{10... | collective-permute-start | bytes 1572872 | tf_op jit(solution)/shard_map/ppermute | solution.py:504
  5.2 1.0 collective-permute-start
  6.2 0.1 sine_convert_fusion
  6.2 0.1 fusion.6
  6.3 0.1 constant_dynamic-slice_fusion
  6.6 0.1 and_select_fusion
  6.7 0.1 broadcast_add_fusion
  7.0 0.2 copy.15.bins_ref
  7.2 0.1 maximum_maximum_fusion.table_ref
  7.4 11.5 %collective-permute-done.1 = bf16[2,32,32,128]{3,2,1,0:T(8,128)(2,1)S(1)} collective-permute-done((bf16[2,32,32,128]{3,2,1,0:T(8,128)(2,1)S(1)}, bf16[2,32,32,128]{3,2,1,0:T(8,128)(2,1)S(1)}, u32[]{:S(2)}, u32[]{:S(2)}) %collective-permute-start.1) | collective-permute-done | bytes 524320 | tf_op jit(solution)/shard_map/ppermute | solution.py:504
  18.9 0.1 pad_maximum_fusion.ext_ref
  19.1 6.9 %snap_gram.2 = (bf16[8,2,32,16,128]{4,3,2,1,0:T(8,128)(2,1)S(1)}, f32[8,48,768]{2,1,0:T(8,128)S(1)}) custom-call(s32[8,16]{1,0:T(8,128)S(1)} %get-tuple-element.28.col_ref, s32[8,16]{1,0:T(8,128)S(1)} %get-tuple-element.26.bins_ref, f32[8,16]{1,0:T(8,128)S(1)} %get-tuple-element.37.cos_ref, f32[8,16]{1,0:T(8,128)S(1)} %get-tuple-element.22.sin_ref, ...), custom_call_target="tpu_custom_call" | custom-call | flops 4800000000 | bytes 12000000 | tf_op jit(solution)/shard_map/snap_gram/pallas_call | solution.py:466
  26.1 3.6 %collective-permute-done = bf16[2,32,32,128]{3,2,1,0:T(8,128)(2,1)} collective-permute-done((bf16[2,32,32,128]{3,2,1,0:T(8,128)(2,1)}, bf16[2,32,32,128]{3,2,1,0:T(8,128)(2,1)}, u32[]{:S(2)}, u32[]{:S(2)}) %collective-permute-start) | collective-permute-done | bytes 524320 | tf_op jit(solution)/shard_map/ppermute | solution.py:505
  29.7 1.2 %pad_maximum_fusion.1.ext_ref = bf16[2,96,32,128]{3,2,1,0:T(8,128)(2,1)S(1)} fusion(bf16[2,32,32,128]{3,2,1,0:T(8,128)(2,1)} %collective-permute-done, bf16[2,64,32,128]{3,2,1,0:T(8,128)(2,1)S(1)} %copy-done.3), kind=kLoop, calls=%fused_computation.1 | loop fusion | flops 786432 | bytes 3145728 | tf_op jit(solution)/shard_map/concatenate | solution.py:511
  30.8 0.1 broadcast_in_dim.11.mask_ref
  30.9 6.9 %snap_gram.3 = (bf16[8,2,32,16,128]{4,3,2,1,0:T(8,128)(2,1)S(1)}, f32[8,48,768]{2,1,0:T(8,128)S(1)}) custom-call(s32[8,16]{1,0:T(8,128)S(1)} %get-tuple-element.27.col_ref, s32[8,16]{1,0:T(8,128)S(1)} %get-tuple-element.25.bins_ref, f32[8,16]{1,0:T(8,128)S(1)} %get-tuple-element.38.cos_ref, f32[8,16]{1,0:T(8,128)S(1)} %get-tuple-element.21.sin_ref, ...), custom_call_target="tpu_custom_call" | custom-call | flops 4800000000 | bytes 12000000 | tf_op jit(solution)/shard_map/snap_gram/pallas_call | solution.py:466
  37.9 1.3 %copy-done.1 = bf16[8,2,32,16,128]{4,3,2,1,0:T(8,128)(2,1)} copy-done((bf16[8,2,32,16,128]{4,3,2,1,0:T(8,128)(2,1)}, bf16[8,2,32,16,128]{4,3,2,1,0:T(8,128)(2,1)S(1)}, u32[]{:S(2)}) %copy-start.1) | copy-done | bytes 2097176
  39.2 28.3 %scatter.1.part_ref = f32[2,48,768]{2,1,0:T(8,128)S(1)} custom-call(f32[4,2,48,768]{3,2,1,0:T(8,128)S(1)} %bitcast.10, f32[4,2,48,768]{3,2,1,0:T(8,128)S(1)} %bitcast.11), custom_call_target="tpu_custom_call" | custom-call | tf_op jit(solution)/shard_map/scatter/pallas_call | solution.py:533
  67.5 8.2 %solve.1 = f32[104,32]{1,0:T(8,128)S(1)} custom-call(f32[2,48,768]{2,1,0:T(8,128)S(1)} %scatter.1.part_ref), custom_call_target="tpu_custom_call" | custom-call | tf_op jit(solution)/shard_map/solve/pallas_call | solution.py:544
  75.8 0.1 select_maximum_fusion.pay_ref
  75.9 1.6 %copy-done.2 = bf16[8,2,32,16,128]{4,3,2,1,0:T(8,128)(2,1)S(1)} copy-done((bf16[8,2,32,16,128]{4,3,2,1,0:T(8,128)(2,1)S(1)}, bf16[8,2,32,16,128]{4,3,2,1,0:T(8,128)(2,1)}, u32[]{:S(2)}) %copy-start.2) | copy-done | bytes 2097176
  77.5 25.8 %apply.1 = f32[16,16,128]{2,1,0:T(8,128)S(1)} custom-call(f32[48,128]{1,0:T(8,128)S(1)} %select_maximum_fusion.pay_ref, s32[16,16,1]{2,1,0:T(8,128)S(1)} %copy.15.bins_ref, bf16[8,2,32,16,128]{4,3,2,1,0:T(8,128)(2,1)S(1)} %get-tuple-element.17.refs_0_, bf16[8,2,32,16,128]{4,3,2,1,0:T(8,128)(2,1)S(1)} %copy-done.2), custom_call_target="tpu_custom_call" | custom-call | tf_op jit(solution)/shard_map/apply/pallas_call | solution.py:571
  103.3 0.7 copy.20
  (27 shorter events, 0.7 us)
Async XLA Ops:
  0.0 6.3 %copy-start = (f32[64,16]{0,1:T(8,128)S(1)}, f32[64,16]{0,1:T(8,128)}, u32[]{:S(2)}) copy-start(f32[64,16]{0,1:T(8,128)} %param.10) | copy-start | bytes 12292
  0.0 18.9 %copy-start.3 = (bf16[2,64,32,128]{3,2,1,0:T(8,128)(2,1)S(1)}, bf16[2,64,32,128]{3,2,1,0:T(8,128)(2,1)}, u32[]{:S(2)}) copy-start(bf16[2,64,32,128]{3,2,1,0:T(8,128)(2,1)} %param.6) | copy-start | bytes 3145732
  0.0 6.5 %copy-start.5 = (s32[64,16]{0,1:T(8,128)S(1)}, s32[64,16]{0,1:T(8,128)}, u32[]{:S(2)}) copy-start(s32[64,16]{0,1:T(8,128)} %param.8) | copy-start | bytes 12292
  0.0 6.5 %copy-start.4 = (s32[64,16]{0,1:T(8,128)S(1)}, s32[64,16]{0,1:T(8,128)}, u32[]{:S(2)}) copy-start(s32[64,16]{0,1:T(8,128)} %param.9) | copy-start | bytes 12292
  0.0 6.6 %copy-start.6 = (s32[64]{0:T(128)S(1)}, s32[64]{0:T(128)}, u32[]{:S(2)}) copy-start(s32[64]{0:T(128)} %param.7) | copy-start | bytes 772
  0.0 6.9 %copy-start.7 = (s32[16,1]{0,1:T(1,128)S(1)}, s32[16,1]{0,1:T(1,128)}, u32[]{:S(2)}) copy-start(s32[16,1]{0,1:T(1,128)} %param.11) | copy-start | bytes 196
  2.2 16.7 %collective-permute-start.1 = (bf16[2,32,32,128]{3,2,1,0:T(8,128)(2,1)S(1)}, bf16[2,32,32,128]{3,2,1,0:T(8,128)(2,1)S(1)}, u32[]{:S(2)}, u32[]{:S(2)}) collective-permute-start(bf16[2,32,32,128]{3,2,1,0:T(8,128)(2,1)S(1)} %get-tuple-element.19), channel_id=1, source_target_pairs={{0,8},{8,16},{16,24},{24,0},{1,9},{9,17},{17,25},{25,1},{2,10},{10... | collective-permute-start | bytes 1572872 | tf_op jit(solution)/shard_map/ppermute | solution.py:504
  5.2 24.5 %collective-permute-start = (bf16[2,32,32,128]{3,2,1,0:T(8,128)(2,1)}, bf16[2,32,32,128]{3,2,1,0:T(8,128)(2,1)}, u32[]{:S(2)}, u32[]{:S(2)}) collective-permute-start(bf16[2,32,32,128]{3,2,1,0:T(8,128)(2,1)} %get-tuple-element.20), channel_id=1, source_target_pairs={{8,0},{16,8},{24,16},{0,24},{9,1},{17,9},{25,17},{1,25},{10,2},{18... | collective-permute-start | bytes 1572872 | tf_op jit(solution)/shard_map/ppermute | solution.py:505
  37.9 1.3 %copy-start.1 = (bf16[8,2,32,16,128]{4,3,2,1,0:T(8,128)(2,1)}, bf16[8,2,32,16,128]{4,3,2,1,0:T(8,128)(2,1)S(1)}, u32[]{:S(2)}) copy-start(bf16[8,2,32,16,128]{4,3,2,1,0:T(8,128)(2,1)S(1)} %get-tuple-element.18.refs_1_) | copy-start | bytes 6291460
  75.9 1.6 %copy-start.2 = (bf16[8,2,32,16,128]{4,3,2,1,0:T(8,128)(2,1)S(1)}, bf16[8,2,32,16,128]{4,3,2,1,0:T(8,128)(2,1)}, u32[]{:S(2)}) copy-start(bf16[8,2,32,16,128]{4,3,2,1,0:T(8,128)(2,1)} %copy-done.1) | copy-start | bytes 6291460
